TPU v7x, 256 devices: a whole 4x4x8 slice. The times are simulated.
256 devices in a mesh: head: 8 (over y, x_lo), seq: 32 (over z, x_hi, core).
Axes of the slice: x: 4 (x_hi: 2, x_lo: 2; x = x_hi * 2 + x_lo), y: 4, z: 8, core: 2. Of those that a mesh axis runs over, the one named last changes fastest.
Arguments:
- query: bfloat16 [32768, 3072], P(('seq', 'head')), may hold values from -9 to 9
- key: bfloat16 [32768, 3072], P(('seq', 'head')), may hold values from -9 to 9
- value: bfloat16 [32768, 3072], P(('seq', 'head')), may hold values from -6 to 6
- grad_out: bfloat16 [32768, 3072], P(('seq', 'head')), may hold values from -6 to 6
- tile_list: int32 [256, 12], replicated, may hold values from 0 to 255, as said below
- tile_count: int32 [256], replicated, may hold values from 1 to 12, as said below
Outputs:
- attn_out: bfloat16 [32768, 3072], P(('seq', 'head'))
- grad_query: bfloat16 [32768, 3072], P(('seq', 'head'))
- grad_key: bfloat16 [32768, 3072], P(('seq', 'head'))
- grad_value: bfloat16 [32768, 3072], P(('seq', 'head'))
Inputs may be any that keep to these rules, and one draw needn't show every extreme that they name: `tile_list`: tile g sits at frame block g // 8, tile row (g // 2) % 4 and tile column g % 2. Row a lists only tiles at most one step from tile a along each of the three tile axes; its first entry is a itself; its first tile_count[a] entries are distinct; entries from tile_count[a] on are to be ignored. `tile_count`: the number of used entries of each row of tile_list.
All inputs are finite; a program needn't handle non-finite values.
Results may differ from a plain program's by a relative error of at most 0.012.
The roundings to bfloat16 on the way count: a program that leaves them out, or rounds other values in their place, can miss the bound.
Values may be sent and summed in bfloat16 or wider, within the bound.
A program may use at most 128 MiB of HBM per device.

v0:
```python
import jax
import jax.numpy as jnp
from jax import lax
from jax.sharding import PartitionSpec as P

HD = 128
TILE = 128
TILES_DEV = 8
SLAB = 1024


def padded(cells, sides, width):
    for axis, dim in sides:
        count = lax.axis_size(axis)
        ends = count - 1
        head = lax.slice_in_dim(cells, 0, width, axis=dim)
        tail = lax.slice_in_dim(cells, cells.shape[dim] - width, cells.shape[dim], axis=dim)
        cells = jnp.concatenate(
            [
                lax.ppermute(tail, axis, [(i, (i + 1) % count) for i in range(ends)]),
                cells,
                lax.ppermute(head, axis, [((i + 1) % count, i) for i in range(ends)]),
            ],
            axis=dim,
        )
    return cells


def passed_along(block, axis, distance):
    devices = range(lax.axis_size(axis))
    route = [(i - distance, i) for i in devices if i - distance in devices]
    return lax.ppermute(block, axis, route)


def tile_scores(query_tiles, key_tiles, scaling):
    return (
        jnp.einsum("tqhd,tkhd->thqk", query_tiles, key_tiles, preferred_element_type=jnp.float32)
        * scaling
    )


def selector(slots, width, dtype):
    return (slots[:, None] == jnp.arange(width, dtype=jnp.int32)[None, :]).astype(dtype)


def pick_tiles(pool, slots):
    chooser = selector(slots, pool.shape[0], pool.dtype)
    picked = jnp.einsum("tp,pkhd->tkhd", chooser, pool, preferred_element_type=jnp.float32)
    return picked.astype(pool.dtype)


def spread_tiles(values, slots, width):
    chooser = selector(slots, width, jnp.float32)
    return jnp.einsum("tp,tkhd->pkhd", chooser, values, precision=lax.Precision.HIGHEST)


def tile_grads(
    query_tiles, cotangent_tiles, key_tiles, value_tiles, log_total, row_delta, in_use, scaling
):
    score = tile_scores(query_tiles, key_tiles, scaling)
    probability = jnp.where(in_use, jnp.exp(score - log_total[..., None]), 0.0)
    prob_b = probability.astype(jnp.bfloat16)
    grad_prob = jnp.einsum(
        "tqhd,tkhd->thqk", cotangent_tiles, value_tiles, preferred_element_type=jnp.float32
    )
    grad_score = (probability * (grad_prob - row_delta[..., None])).astype(jnp.bfloat16)
    key_grad = jnp.einsum(
        "thqk,tqhd->tkhd", grad_score, query_tiles, preferred_element_type=jnp.float32
    )
    value_grad = jnp.einsum(
        "thqk,tqhd->tkhd", prob_b, cotangent_tiles, preferred_element_type=jnp.float32
    )
    return (grad_score, key_grad, value_grad)


def per_device(query, key, value, grad_out, tile_list, tile_count):
    scaling = HD ** (-0.5)
    slab_index = lax.axis_index("seq")
    query_heads, key_heads, value_heads, cotangent_heads = (
        lax.all_to_all(query, "head", split_axis=1, concat_axis=0, tiled=True),
        lax.all_to_all(key, "head", split_axis=1, concat_axis=0, tiled=True),
        lax.all_to_all(value, "head", split_axis=1, concat_axis=0, tiled=True),
        lax.all_to_all(grad_out, "head", split_axis=1, concat_axis=0, tiled=True),
    )
    columns = query_heads.shape[1]
    heads_dev = columns // HD
    tile_shape = (TILES_DEV, TILE, heads_dev, HD)
    query_tiles = query_heads.reshape(tile_shape)
    key_value = jnp.stack([key_heads, value_heads])
    with_rims = padded(key_value, (("seq", 1),), SLAB)
    kv_pool = with_rims.reshape(2, 3 * TILES_DEV, TILE, heads_dev, HD)
    keys_pool = kv_pool[0]
    values_pool = kv_pool[1]
    pool_width = 3 * TILES_DEV
    own_list = lax.dynamic_slice_in_dim(tile_list, slab_index * TILES_DEV, TILES_DEV, 0)
    own_count = lax.dynamic_slice_in_dim(tile_count, slab_index * TILES_DEV, TILES_DEV, 0)
    pool_slots = (own_list // TILES_DEV - slab_index + 1) * TILES_DEV + own_list % TILES_DEV
    busiest = jnp.max(own_count)

    def norm_pass(slot_index, running):
        running_max, row_total = running
        picked = lax.dynamic_index_in_dim(pool_slots, slot_index, 1, keepdims=False)
        score = tile_scores(query_tiles, pick_tiles(keys_pool, picked), scaling)
        in_use = (slot_index < own_count)[:, None, None]
        new_max = jnp.where(in_use, jnp.maximum(running_max, jnp.max(score, axis=3)), running_max)
        added = jnp.where(in_use, jnp.sum(jnp.exp(score - new_max[..., None]), axis=3), 0.0)
        return (new_max, row_total * jnp.exp(running_max - new_max) + added)

    stat_shape = (TILES_DEV, heads_dev, TILE)
    running_max, row_total = lax.fori_loop(
        0,
        busiest,
        norm_pass,
        (jnp.full(stat_shape, -jnp.inf, jnp.float32), jnp.zeros(stat_shape, jnp.float32)),
    )
    log_total = running_max + jnp.log(row_total)

    def value_pass(slot_index, accum):
        picked = lax.dynamic_index_in_dim(pool_slots, slot_index, 1, keepdims=False)
        score = tile_scores(query_tiles, pick_tiles(keys_pool, picked), scaling)
        in_use = (slot_index < own_count)[:, None, None, None]
        prob_b = jnp.where(in_use, jnp.exp(score - log_total[..., None]), 0.0).astype(jnp.bfloat16)
        return accum + jnp.einsum(
            "thqk,tkhd->tqhd",
            prob_b,
            pick_tiles(values_pool, picked),
            preferred_element_type=jnp.float32,
        )

    attn_tiles = lax.fori_loop(0, busiest, value_pass, jnp.zeros(tile_shape, jnp.float32)).astype(
        jnp.bfloat16
    )
    attn_heads = attn_tiles.reshape(SLAB, columns)
    attn_out = lax.all_to_all(attn_heads, "head", split_axis=0, concat_axis=1, tiled=True)
    cotangent_tiles = cotangent_heads.reshape(tile_shape)
    attn_wide = lax.optimization_barrier(attn_tiles).astype(jnp.float32)
    row_delta = jnp.transpose(
        jnp.sum(cotangent_tiles.astype(jnp.float32) * attn_wide, axis=3), (0, 2, 1)
    )

    def backward_pass(slot_index, carried):
        grad_accum, pool_key, pool_value = carried
        picked = lax.dynamic_index_in_dim(pool_slots, slot_index, 1, keepdims=False)
        key_tiles = pick_tiles(keys_pool, picked)
        in_use = (slot_index < own_count)[:, None, None, None]
        grad_score, key_grad, value_grad = tile_grads(
            query_tiles,
            cotangent_tiles,
            key_tiles,
            pick_tiles(values_pool, picked),
            log_total,
            row_delta,
            in_use,
            scaling,
        )
        grad_accum = grad_accum + jnp.einsum(
            "thqk,tkhd->tqhd", grad_score, key_tiles, preferred_element_type=jnp.float32
        )
        pool_key = pool_key + spread_tiles(key_grad, picked, pool_width)
        pool_value = pool_value + spread_tiles(value_grad, picked, pool_width)
        return (grad_accum, pool_key, pool_value)

    empty_pool = jnp.zeros((pool_width,) + tile_shape[1:], jnp.float32)
    grad_accum, pool_key, pool_value = lax.fori_loop(
        0, busiest, backward_pass, (jnp.zeros(tile_shape, jnp.float32), empty_pool, empty_pool)
    )
    own_key = pool_key[TILES_DEV : 2 * TILES_DEV]
    own_value = pool_value[TILES_DEV : 2 * TILES_DEV]
    lower_part = jnp.stack([pool_key[:TILES_DEV], pool_value[:TILES_DEV]]).astype(jnp.bfloat16)
    upper_part = jnp.stack([pool_key[2 * TILES_DEV :], pool_value[2 * TILES_DEV :]]).astype(
        jnp.bfloat16
    )
    from_below = passed_along(upper_part, "seq", 1).astype(jnp.float32)
    from_above = passed_along(lower_part, "seq", -1).astype(jnp.float32)
    grad_key_sum = own_key + from_below[0] + from_above[0]
    grad_value_sum = own_value + from_below[1] + from_above[1]
    query_grad = (scaling * grad_accum).astype(jnp.bfloat16).reshape(SLAB, columns)
    key_grad_out = (scaling * grad_key_sum).astype(jnp.bfloat16).reshape(SLAB, columns)
    value_grad_out = grad_value_sum.astype(jnp.bfloat16).reshape(SLAB, columns)
    grad_query, grad_key, grad_value = (
        lax.all_to_all(query_grad, "head", split_axis=0, concat_axis=1, tiled=True),
        lax.all_to_all(key_grad_out, "head", split_axis=0, concat_axis=1, tiled=True),
        lax.all_to_all(value_grad_out, "head", split_axis=0, concat_axis=1, tiled=True),
    )
    return (attn_out, grad_query, grad_key, grad_value)


def solution(mesh):
    placed = (
        P(("seq", "head"), None),
        P(("seq", "head"), None),
        P(("seq", "head"), None),
        P(("seq", "head"), None),
        P(),
        P(),
    )
    return jax.shard_map(
        per_device,
        mesh=mesh,
        in_specs=placed,
        out_specs=(
            P(("seq", "head"), None),
            P(("seq", "head"), None),
            P(("seq", "head"), None),
            P(("seq", "head"), None),
        ),
        check_vma=False,
    )
```

profile of v0, /device:TPU:1, one launch (start us, length us, event | category | flops | bytes accessed | tf_op | source)
XLA Modules:
  0.0 647.6 jit_solution(8043777818952585101)
XLA Ops:
  3.3 5.9 all-to-all-start
  10.8 10.1 %all-to-all-done = bf16[128,8,384]{2,0,1:T(8,128)(2,1)S(1)} async-done(((bf16[128,8,384]{2,0,1:T(8,128)(2,1)}), bf16[128,8,384]{2,0,1:T(8,128)(2,1)S(1)}, u32[]{:S(2)}, u32[]{:S(2)}) %all-to-all-start) | async-done | bytes 786464 | tf_op jit(solution)/shard_map/all_to_all | solution.py:81
  25.0 10.9 %all-to-all-done.1 = bf16[128,8,384]{2,0,1:T(8,128)(2,1)S(1)} async-done(((bf16[128,8,384]{2,0,1:T(8,128)(2,1)}), bf16[128,8,384]{2,0,1:T(8,128)(2,1)S(1)}, u32[]{:S(2)}, u32[]{:S(2)}) %all-to-all-start.1) | async-done | bytes 786464 | tf_op jit(solution)/shard_map/all_to_all | solution.py:82
  37.5 4.8 collective-permute-start.1
  52.5 39.9 %all-to-all-done.2 = bf16[128,8,384]{0,2,1:T(8,128)(2,1)S(1)} async-done(((bf16[128,8,384]{0,2,1:T(8,128)(2,1)}), bf16[128,8,384]{0,2,1:T(8,128)(2,1)S(1)}, u32[]{:S(2)}, u32[]{:S(2)}) %all-to-all-start.2) | async-done | bytes 786464 | tf_op jit(solution)/shard_map/all_to_all | solution.py:80
  98.3 6.6 %all-to-all-done.4 = bf16[128,8,384]{0,2,1:T(8,128)(2,1)S(1)} async-done(((bf16[128,8,384]{0,2,1:T(8,128)(2,1)}), bf16[128,8,384]{0,2,1:T(8,128)(2,1)S(1)}, u32[]{:S(2)}, u32[]{:S(2)}) %all-to-all-start.4) | async-done | bytes 786464 | tf_op jit(solution)/shard_map/all_to_all | solution.py:83
  115.7 28.3 %while.36 = (s32[]{:T(128)}, f32[8,3,128]{2,1,0:T(4,128)S(1)}, f32[8,3,128]{2,1,0:T(4,128)S(1)}, s32[]{:T(128)}, s32[8]{0:T(128)S(1)}, /*index=5*/s32[8,12]{0,1:...) while((s32[]{:T(128)}, f32[8,3,128]{2,1,0:T(4,128)S(1)}, ...), condition=%wide.region_4.5_spmd, body=%wide.region_1.4_spmd.sunk | while | flops 121516232 | bytes 8024375 | solution.py:110
  147.7 4.7 copy.79
  153.8 96.1 %while.37 = (s32[]{:T(128)}, f32[8,128,3,128]{1,3,2,0:T(8,128)}, s32[]{:T(128)}, s32[8,12]{0,1:T(8,128)S(1)}, bf16[24,128,3,128]{3,0,2,1:T(8,128)(2,1)}, /*index...) while((s32[]{:T(128)}, f32[8,128,3,128]{1,3,2,0:T(8,128)}, ...), condition=%wide.region_6.7_spmd, body=%wide.region_5.6_spmd.sunk | while | flops 241828240 | bytes 21246324 | solution.py:130
  260.2 285.3 %while.38 = (s32[]{:T(128)}, f32[8,128,3,128]{1,3,2,0:T(8,128)}, f32[24,128,3,128]{3,0,2,1:T(8,128)}, f32[24,128,3,128]{3,0,2,1:T(8,128)}, s32[]{:T(128)}, /*ind...) while((s32[]{:T(128)}, f32[8,128,3,128]{1,3,2,0:T(8,128)}, ...), condition=%wide.region_9.10_spmd, body=%wide.region_8.9_spmd.sunk | while | flops 773849856 | bytes 136864496 | solution.py:164
  273.3 4.3 convolution_add_fusion.4
  277.6 4.3 convolution_add_fusion.5
  297.0 4.3 convolution_add_fusion.4
  301.3 4.3 convolution_add_fusion.5
  320.6 4.3 convolution_add_fusion.4
  325.0 4.3 convolution_add_fusion.5
  344.3 4.3 convolution_add_fusion.4
  348.7 4.3 convolution_add_fusion.5
  368.0 4.3 convolution_add_fusion.4
  372.4 4.3 convolution_add_fusion.5
  415.4 4.3 convolution_add_fusion.4
  439.1 4.3 convolution_add_fusion.4
  443.5 4.3 convolution_add_fusion.5
  462.8 4.3 convolution_add_fusion.4
  467.2 4.3 convolution_add_fusion.5
  490.9 4.3 convolution_add_fusion.5
  514.6 4.3 convolution_add_fusion.5
  545.5 6.1 copy.91
  554.4 6.1 copy.89
  568.1 5.3 collective-permute-start.2
  578.3 25.4 %all-to-all-done.3 = bf16[8,128,384]{1,2,0:T(8,128)(2,1)S(1)} async-done(((bf16[8,128,384]{1,2,0:T(8,128)(2,1)}), bf16[8,128,384]{1,2,0:T(8,128)(2,1)S(1)}, u32[]{:S(2)}, u32[]{:S(2)}) %all-to-all-start.3) | async-done | bytes 786464 | tf_op jit(solution)/shard_map/all_to_all | solution.py:134
  624.1 9.5 %all-to-all-done.6 = bf16[8,128,384]{2,1,0:T(8,128)(2,1)S(1)} async-done(((bf16[8,128,384]{2,1,0:T(8,128)(2,1)}), bf16[8,128,384]{2,1,0:T(8,128)(2,1)S(1)}, u32[]{:S(2)}, u32[]{:S(2)}) %all-to-all-start.6) | async-done | bytes 786464 | tf_op jit(solution)/shard_map/all_to_all | solution.py:182
  (680 shorter events, 412.8 us)
Async XLA Ops:
  2.1 7.1 %copy-start.15 = (bf16[128,3072]{1,0:T(8,128)(2,1)S(1)}, bf16[128,3072]{1,0:T(8,128)(2,1)}, u32[]{:S(2)}) copy-start(bf16[128,3072]{1,0:T(8,128)(2,1)} %param.14) | copy-start | bytes 2359300
  3.3 17.6 %all-to-all-start = ((bf16[128,8,384]{2,0,1:T(8,128)(2,1)}), bf16[128,8,384]{2,0,1:T(8,128)(2,1)S(1)}, u32[]{:S(2)}, u32[]{:S(2)}) async-start(bf16[128,8,384]{2,0,1:T(8,128)(2,1)} %copy.71), calls=%async_computation | async-start | bytes 1572864 | tf_op jit(solution)/shard_map/all_to_all | solution.py:81
  20.9 15.0 %all-to-all-start.1 = ((bf16[128,8,384]{2,0,1:T(8,128)(2,1)}), bf16[128,8,384]{2,0,1:T(8,128)(2,1)S(1)}, u32[]{:S(2)}, u32[]{:S(2)}) async-start(bf16[128,8,384]{2,0,1:T(8,128)(2,1)} %copy.73), calls=%async_computation.1 | async-start | bytes 1572864 | tf_op jit(solution)/shard_map/all_to_all | solution.py:82
  36.2 10.4 %copy-start.16 = (bf16[128,3072]{1,0:T(8,128)(2,1)S(1)}, bf16[128,3072]{1,0:T(8,128)(2,1)}, u32[]{:S(2)}) copy-start(bf16[128,3072]{1,0:T(8,128)(2,1)} %param.12) | copy-start | bytes 2359300
  37.5 13.8 %copy-start.17 = (bf16[128,3072]{1,0:T(8,128)(2,1)S(1)}, bf16[128,3072]{1,0:T(8,128)(2,1)}, u32[]{:S(2)}) copy-start(bf16[128,3072]{1,0:T(8,128)(2,1)} %param.15) | copy-start | bytes 2359300
  37.5 68.6 %collective-permute-start.1 = (bf16[2,1024,384]{1,2,0:T(8,128)(2,1)}, bf16[2,1024,384]{1,2,0:T(8,128)(2,1)}, u32[]{:S(2)}, u32[]{:S(2)}) collective-permute-start(bf16[2,1024,384]{1,2,0:T(8,128)(2,1)} %pad_maximum_fusion.1), channel_id=1, source_target_pairs={{1,0},{2,1},{3,2},{4,3},{5,4},{6,5},{7,6},{8,7},{9,8},{10,9},{11,1... | collective-permute-start | bytes 4718600 | tf_op jit(solution)/shard_map/ppermute | solution.py:22
  42.3 63.8 %collective-permute-start = (bf16[2,1024,384]{1,2,0:T(8,128)(2,1)}, bf16[2,1024,384]{1,2,0:T(8,128)(2,1)}, u32[]{:S(2)}, u32[]{:S(2)}) collective-permute-start(bf16[2,1024,384]{1,2,0:T(8,128)(2,1)} %pad_maximum_fusion.1), channel_id=1, source_target_pairs={{0,1},{1,2},{2,3},{3,4},{4,5},{5,6},{6,7},{7,8},{8,9},{9,10},{10,1... | collective-permute-start | bytes 4718600 | tf_op jit(solution)/shard_map/ppermute | solution.py:20
  47.8 44.7 %all-to-all-start.2 = ((bf16[128,8,384]{0,2,1:T(8,128)(2,1)}), bf16[128,8,384]{0,2,1:T(8,128)(2,1)S(1)}, u32[]{:S(2)}, u32[]{:S(2)}) async-start(bf16[128,8,384]{0,2,1:T(8,128)(2,1)} %bitcast.22), calls=%async_computation.2 | async-start | bytes 1572864 | tf_op jit(solution)/shard_map/all_to_all | solution.py:80
  51.3 44.7 %copy-start.19 = (s32[256]{0:T(256)S(1)}, s32[256]{0:T(256)}, u32[]{:S(2)}) copy-start(s32[256]{0:T(256)} %param.17) | copy-start | bytes 3076
  51.3 45.4 %copy-start.18 = (s32[256,12]{0,1:T(8,128)S(1)}, s32[256,12]{0,1:T(8,128)}, u32[]{:S(2)}) copy-start(s32[256,12]{0,1:T(8,128)} %param.16) | copy-start | bytes 36868
  92.5 12.5 %all-to-all-start.4 = ((bf16[128,8,384]{0,2,1:T(8,128)(2,1)}), bf16[128,8,384]{0,2,1:T(8,128)(2,1)S(1)}, u32[]{:S(2)}, u32[]{:S(2)}) async-start(bf16[128,8,384]{0,2,1:T(8,128)(2,1)} %bitcast.208), calls=%async_computation.4 | async-start | bytes 1572864 | tf_op jit(solution)/shard_map/all_to_all | solution.py:83
  272.1 5.5 slice-start
  295.8 5.5 slice-start
  319.5 5.5 slice-start
  343.2 5.5 slice-start
  366.9 5.5 slice-start
  390.6 5.5 slice-start
  414.3 5.5 slice-start
  438.0 5.5 slice-start
  461.6 5.5 slice-start
  485.3 5.5 slice-start
  509.0 5.5 slice-start
  532.7 5.5 slice-start
  564.8 43.1 %collective-permute-start.3 = (bf16[2,8,128,3,128]{2,4,3,1,0:T(8,128)(2,1)}, bf16[2,8,128,3,128]{2,4,3,1,0:T(8,128)(2,1)}, u32[]{:S(2)}, u32[]{:S(2)}) collective-permute-start(bf16[2,8,128,3,128]{2,4,3,1,0:T(8,128)(2,1)} %pad_maximum_fusion.3), channel_id=1, source_target_pairs={{1,0},{2,1},{3,2},{4,3},{5,4},{6,5},{7,6},{8,7},{9,8},{10,9},{11,1... | collective-permute-start | bytes 4718600 | tf_op jit(solution)/shard_map/ppermute | solution.py:32
  568.1 8.8 %copy-start.8 = (f32[8,128,3,128]{1,3,2,0:T(8,128)S(1)}, f32[8,128,3,128]{1,3,2,0:T(8,128)}, u32[]{:S(2)}) copy-start(f32[8,128,3,128]{1,3,2,0:T(8,128)} %get-tuple-element.169) | copy-start | bytes 4718596
  568.1 41.7 %collective-permute-start.2 = (bf16[2,8,128,3,128]{2,4,3,1,0:T(8,128)(2,1)}, bf16[2,8,128,3,128]{2,4,3,1,0:T(8,128)(2,1)}, u32[]{:S(2)}, u32[]{:S(2)}) collective-permute-start(bf16[2,8,128,3,128]{2,4,3,1,0:T(8,128)(2,1)} %pad_maximum_fusion.2), channel_id=1, source_target_pairs={{0,1},{1,2},{2,3},{3,4},{4,5},{5,6},{6,7},{7,8},{8,9},{9,10},{10,1... | collective-permute-start | bytes 4718600 | tf_op jit(solution)/shard_map/ppermute | solution.py:32
  573.3 30.3 %all-to-all-start.3 = ((bf16[8,128,384]{1,2,0:T(8,128)(2,1)}), bf16[8,128,384]{1,2,0:T(8,128)(2,1)S(1)}, u32[]{:S(2)}, u32[]{:S(2)}) async-start(bf16[8,128,384]{1,2,0:T(8,128)(2,1)} %bitcast.26), calls=%async_computation.3 | async-start | bytes 1572864 | tf_op jit(solution)/shard_map/all_to_all | solution.py:134
  603.7 15.3 %all-to-all-start.5 = ((bf16[8,128,384]{2,1,0:T(8,128)(2,1)}), bf16[8,128,384]{2,1,0:T(8,128)(2,1)}, u32[]{:S(2)}, u32[]{:S(2)}) async-start(bf16[8,128,384]{2,1,0:T(8,128)(2,1)} %copy.87), calls=%async_computation.5 | async-start | bytes 1572864 | tf_op jit(solution)/shard_map/all_to_all | solution.py:181
  615.5 7.4 %copy-start.14 = (bf16[8,128,3,128]{1,3,2,0:T(8,128)(2,1)S(1)}, bf16[8,128,3,128]{1,3,2,0:T(8,128)(2,1)}, u32[]{:S(2)}) copy-start(bf16[8,128,3,128]{1,3,2,0:T(8,128)(2,1)} %get-tuple-element.355) | copy-start | bytes 2359300
  618.9 14.6 %all-to-all-start.6 = ((bf16[8,128,384]{2,1,0:T(8,128)(2,1)}), bf16[8,128,384]{2,1,0:T(8,128)(2,1)S(1)}, u32[]{:S(2)}, u32[]{:S(2)}) async-start(bf16[8,128,384]{2,1,0:T(8,128)(2,1)} %copy.92), calls=%async_computation.6 | async-start | bytes 1572864 | tf_op jit(solution)/shard_map/all_to_all | solution.py:182
  622.9 14.2 %copy-start.12 = (bf16[8,128,384]{1,2,0:T(8,128)(2,1)S(1)}, bf16[8,128,384]{1,2,0:T(8,128)(2,1)}, u32[]{:S(2)}) copy-start(bf16[8,128,384]{1,2,0:T(8,128)(2,1)} %copy-done.11) | copy-start | bytes 2359300
  633.6 12.5 %all-to-all-start.7 = ((bf16[8,128,384]{2,1,0:T(8,128)(2,1)}), bf16[8,128,384]{2,1,0:T(8,128)(2,1)S(1)}, u32[]{:S(2)}, u32[]{:S(2)}) async-start(bf16[8,128,384]{2,1,0:T(8,128)(2,1)} %copy.95), calls=%async_computation.7 | async-start | bytes 1572864 | tf_op jit(solution)/shard_map/all_to_all | solution.py:183
  (136 other events, 312.0 us)
where the time goes:
time: 651 us; the launch traced here: 648 us
  matrix products  301 us (46%)
  local copies, waits for them, and re-layouts  135 us (21%)
  waiting for transfers between devices  107 us (16%)
  starting transfers between devices  48.4 us (7%)
  other arithmetic  30 us (5%)
  loops' own time  25.1 us (4%)
    dot_general x24, matrix products, spread_tiles(): jnp.einsum('tp,tkhd->pkhd', chooser, values, precision=lax.Precision.HIGH...  103 us
    dot_general x60, matrix products, pick_tiles(): jnp.einsum('tp,pkhd->tkhd', chooser, pool, preferred_element_type=jnp.flo...  94.9 us
    while x300, local copies, waits for them, and re-layouts  48.6 us
    dot_general x12, matrix products, value_pass(): jnp.einsum('thqk,tkhd->tqhd', prob_b, pick_tiles(values_pool, picked), pr...  48 us
    all_to_all x1, waiting for transfers between devices, per_device(): lax.all_to_all(query, 'head', split_axis=1, concat_axis=0, tiled=True)  39.9 us
    dot_general x24, matrix products, tile_scores(): jnp.einsum('tqhd,tkhd->thqk', query_tiles, key_tiles, preferred_element_t...  31.6 us
    convert_element_type x12, local copies, waits for them, and re-layouts, pick_tiles(): return picked.astype(pool.dtype)  28.9 us
    all_to_all x1, waiting for transfers between devices, per_device(): lax.all_to_all(attn_heads, 'head', split_axis=0, concat_axis=1, tiled=True)  25.4 us
  transfers between devices with their start and end apart: 12, of which 8 were waited for; matrix products, arithmetic and copies ran while one was open for 4% of the time, Pallas kernels for 0%

commit v1 on v0

v1 whole, which is shorter than its diff:
```python
import functools

import jax
import jax.numpy as jnp
from jax import lax
from jax.experimental import pallas as pl
from jax.experimental.pallas import tpu as pltpu
from jax.sharding import PartitionSpec as P

HD = 128
TILE = 128
TILES_DEV = 8
SLAB = 1024
LIST = 12
GROUP = 4
CHUNKS = LIST // GROUP
SCALING = HD ** (-0.5)
LOG2E = 1.4426950408889634
UNUSED = 1e30


def attention_kernel(
    heads, list_hbm, count_ref, q_hbm, g_hbm, kp_hbm, vp_hbm,
    o_hbm, dq_hbm, low_hbm, up_hbm, own_hbm,
    list_ref, q_ref, g_ref, kp_ref, vp_ref, w_ref, e_ref, dp_ref, stat_ref, ot_ref, dqt_ref,
    acc_ref, o_ref, dq_ref, low_ref, up_ref, own_ref, in_sem, out_sem,
):
    slab = lax.axis_index("seq")
    loads = [
        pltpu.make_async_copy(src, dst, in_sem.at[i])
        for i, (src, dst) in enumerate(
            [
                (list_hbm.at[pl.ds(pl.multiple_of(slab * TILES_DEV, TILES_DEV), TILES_DEV)], list_ref),
                (kp_hbm, kp_ref),
                (vp_hbm, vp_ref),
                (q_hbm, q_ref),
                (g_hbm, g_ref),
            ]
        )
    ]
    for load in loads:
        load.start()
    w_ref[...] = jnp.zeros_like(w_ref)

    def clear(slot, _):
        acc_ref[slot] = jnp.zeros(acc_ref.shape[1:], jnp.float32)
        return 0

    lax.fori_loop(0, 3 * TILES_DEV, clear, 0)
    for load in loads:
        load.wait()

    def columns(h):
        return slice(h * HD, (h + 1) * HD)

    def query_tile(a, _):
        used = count_ref[slab * TILES_DEV + a]
        chunks = (used + (GROUP - 1)) // GROUP
        for h in range(heads):
            w_ref[h, :TILE, :HD] = g_ref[a, :, columns(h)]
            w_ref[h, TILE:, HD:] = q_ref[a, :, columns(h)]
        ot_ref[...] = jnp.zeros_like(ot_ref)
        dqt_ref[...] = jnp.zeros_like(dqt_ref)
        for c in range(CHUNKS):
            stat_ref[c] = jnp.full(stat_ref.shape[1:], -UNUSED, jnp.float32)

        def slots_of(c):
            slots, extra = [], []
            for u in range(GROUP):
                j = c * GROUP + u
                valid = j < used
                slots.append(list_ref[a, jnp.where(valid, j, 0)] - (slab - 1) * TILES_DEV)
                extra.append(jnp.where(valid, 0.0, UNUSED).astype(jnp.float32))
            return slots, extra

        def scores(c, _):
            slots, extra = slots_of(c)
            for h in range(heads):
                pairs = jnp.concatenate(
                    [
                        jnp.concatenate([vp_ref[s, :, columns(h)], kp_ref[s, :, columns(h)]], axis=1)
                        for s in slots
                    ],
                    axis=0,
                )
                both = lax.dot_general(
                    pairs, w_ref[h], (((1,), (1,)), ((), ())), preferred_element_type=jnp.float32
                )
                grad_prob = both[:, :TILE]
                score = both[:, TILE:]
                top = jnp.max(score, axis=0, keepdims=True)
                total = jnp.zeros((1, TILE), jnp.float32)
                dots = jnp.zeros((1, TILE), jnp.float32)
                for u in range(GROUP):
                    rows = slice(u * TILE, (u + 1) * TILE)
                    e = jnp.exp2((score[rows] - (top + extra[u])) * (SCALING * LOG2E))
                    e_ref[c, h, rows] = e
                    total = total + jnp.sum(e, axis=0, keepdims=True)
                    dots = dots + jnp.sum(e * grad_prob[rows], axis=0, keepdims=True)
                dp_ref[c, h] = grad_prob
                stat_ref[c, h, 0:1] = top
                stat_ref[c, h, 1:2] = total
                stat_ref[c, h, 2:3] = dots
            return 0

        lax.fori_loop(0, chunks, scores, 0)

        for h in range(heads):
            top = functools.reduce(jnp.maximum, [stat_ref[c, h, 0:1] for c in range(CHUNKS)])
            total = jnp.zeros((1, TILE), jnp.float32)
            dots = jnp.zeros((1, TILE), jnp.float32)
            weights = []
            for c in range(CHUNKS):
                weight = jnp.exp2((stat_ref[c, h, 0:1] - top) * (SCALING * LOG2E))
                total = total + weight * stat_ref[c, h, 1:2]
                dots = dots + weight * stat_ref[c, h, 2:3]
                weights.append(weight)
            inverse = 1.0 / total
            for c in range(CHUNKS):
                stat_ref[c, h, 3:4] = weights[c] * inverse
            stat_ref[0, h, 4:5] = dots * inverse

        def grads(c, _):
            slots, _ = slots_of(c)
            for h in range(heads):
                factor = stat_ref[c, h, 3:4]
                delta = stat_ref[0, h, 4:5]
                p = e_ref[c, h] * factor
                ds = (p * (dp_ref[c, h] - delta)).astype(jnp.bfloat16)
                pb = p.astype(jnp.bfloat16)
                keys = jnp.concatenate([kp_ref[s, :, columns(h)] for s in slots], axis=0)
                values = jnp.concatenate([vp_ref[s, :, columns(h)] for s in slots], axis=0)
                both = lax.dot_general(
                    jnp.concatenate([pb, ds], axis=1), w_ref[h], (((1,), (0,)), ((), ())),
                    preferred_element_type=jnp.float32,
                )
                for u in range(GROUP):
                    acc_ref[slots[u], :, 2 * h * HD : 2 * (h + 1) * HD] += both[u * TILE : (u + 1) * TILE]
                ot_ref[h] += lax.dot_general(
                    values, pb, (((0,), (0,)), ((), ())), preferred_element_type=jnp.float32
                )
                dqt_ref[h] += lax.dot_general(
                    keys, ds, (((0,), (0,)), ((), ())), preferred_element_type=jnp.float32
                )
            return 0

        lax.fori_loop(0, chunks, grads, 0)
        for h in range(heads):
            o_ref[a, :, columns(h)] = ot_ref[h].T.astype(jnp.bfloat16)
            dq_ref[a, :, columns(h)] = (dqt_ref[h].T * SCALING).astype(jnp.bfloat16)
        return 0

    lax.fori_loop(0, TILES_DEV, query_tile, 0)

    stores = [
        pltpu.make_async_copy(src, dst, out_sem.at[i])
        for i, (src, dst) in enumerate(
            [(o_ref, o_hbm), (dq_ref, dq_hbm), (low_ref, low_hbm), (up_ref, up_hbm), (own_ref, own_hbm)]
        )
    ]
    stores[0].start()
    stores[1].start()

    def finish(t, _):
        for h in range(heads):
            for kind in range(2):
                part = slice((2 * h + 1 - kind) * HD, (2 * h + 2 - kind) * HD)
                low_ref[kind, t, :, columns(h)] = acc_ref[t, :, part].astype(jnp.bfloat16)
                up_ref[kind, t, :, columns(h)] = acc_ref[2 * TILES_DEV + t, :, part].astype(jnp.bfloat16)
                own_ref[kind, t, :, columns(h)] = acc_ref[TILES_DEV + t, :, part]
        return 0

    lax.fori_loop(0, TILES_DEV, finish, 0)
    for store in stores[2:]:
        store.start()
    for store in stores:
        store.wait()


def attention(tile_list, tile_count, query, cotangent, key_pool, value_pool):
    columns = query.shape[2]
    heads = columns // HD
    own = (TILES_DEV, TILE, columns)
    pool = (3 * TILES_DEV, TILE, columns)
    pair = (2,) + own
    hbm = pl.BlockSpec(memory_space=pl.ANY)
    outs = (
        jax.ShapeDtypeStruct(own, jnp.bfloat16),
        jax.ShapeDtypeStruct(own, jnp.bfloat16),
        jax.ShapeDtypeStruct(pair, jnp.bfloat16),
        jax.ShapeDtypeStruct(pair, jnp.bfloat16),
        jax.ShapeDtypeStruct(pair, jnp.float32),
    )
    wide = (CHUNKS, heads, GROUP * TILE, TILE)
    return pl.pallas_call(
        functools.partial(attention_kernel, heads),
        out_shape=outs,
        in_specs=[hbm, pl.BlockSpec(memory_space=pltpu.SMEM), hbm, hbm, hbm, hbm],
        out_specs=(hbm,) * 5,
        scratch_shapes=[
            pltpu.SMEM((TILES_DEV, LIST), jnp.int32),
            pltpu.VMEM(own, jnp.bfloat16),
            pltpu.VMEM(own, jnp.bfloat16),
            pltpu.VMEM(pool, jnp.bfloat16),
            pltpu.VMEM(pool, jnp.bfloat16),
            pltpu.VMEM((heads, 2 * TILE, 2 * HD), jnp.bfloat16),
            pltpu.VMEM(wide, jnp.float32),
            pltpu.VMEM(wide, jnp.float32),
            pltpu.VMEM((CHUNKS, heads, 8, TILE), jnp.float32),
            pltpu.VMEM((heads, HD, TILE), jnp.float32),
            pltpu.VMEM((heads, HD, TILE), jnp.float32),
            pltpu.VMEM((3 * TILES_DEV, TILE, 2 * columns), jnp.float32),
            pltpu.VMEM(own, jnp.bfloat16),
            pltpu.VMEM(own, jnp.bfloat16),
            pltpu.VMEM(pair, jnp.bfloat16),
            pltpu.VMEM(pair, jnp.bfloat16),
            pltpu.VMEM(pair, jnp.float32),
            pltpu.SemaphoreType.DMA((5,)),
            pltpu.SemaphoreType.DMA((5,)),
        ],
        compiler_params=pltpu.CompilerParams(vmem_limit_bytes=56 * 2**20),
        name="attention",
    )(tile_list, tile_count, query, cotangent, key_pool, value_pool)


def with_rims(cells):
    count = lax.axis_size("seq")
    ring = range(count)
    return jnp.concatenate(
        [
            lax.ppermute(cells, "seq", [(i, (i + 1) % count) for i in ring]),
            cells,
            lax.ppermute(cells, "seq", [((i + 1) % count, i) for i in ring]),
        ],
        axis=0,
    )


def per_device(query, key, value, grad_out, tile_list, tile_count):
    def gathered(cells):
        moved = lax.all_to_all(cells, "head", split_axis=1, concat_axis=0, tiled=True)
        return moved.reshape(TILES_DEV, TILE, moved.shape[1])

    def returned(cells):
        return lax.all_to_all(cells.reshape(SLAB, -1), "head", split_axis=0, concat_axis=1, tiled=True)

    key_pool = with_rims(gathered(key))
    value_pool = with_rims(gathered(value))
    out, dq, low, up, own = attention(
        tile_list, tile_count, gathered(query), gathered(grad_out), key_pool, value_pool
    )
    count = lax.axis_size("seq")
    ring = range(count)
    from_below = lax.ppermute(up, "seq", [(i, (i + 1) % count) for i in ring])
    from_above = lax.ppermute(low, "seq", [((i + 1) % count, i) for i in ring])
    total = own + from_below.astype(jnp.float32) + from_above.astype(jnp.float32)
    dk = (SCALING * total[0]).astype(jnp.bfloat16)
    dv = total[1].astype(jnp.bfloat16)
    return returned(out), returned(dq), returned(dk), returned(dv)


def solution(mesh):
    tokens = P(("seq", "head"), None)
    return jax.shard_map(
        per_device,
        mesh=mesh,
        in_specs=(tokens, tokens, tokens, tokens, P(), P()),
        out_specs=(tokens, tokens, tokens, tokens),
        check_vma=False,
    )
```

time: 651 us -> 218 us (0.33)
  the two profiles are of different devices: /device:TPU:1 before, /device:TPU:225 now
where the time goes in v1:
time: 218 us; the launch traced here: 217 us
  waiting for transfers between devices  67.4 us (31%)
  blocking collectives  49.9 us (23%)
  starting transfers between devices  46.7 us (21%)
  local copies, waits for them, and re-layouts  23.1 us (11%)
  Pallas kernels  18.3 us (8%)
  other arithmetic  10.6 us (5%)
    all_to_all x1, blocking collectives, returned(): lax.all_to_all(cells.reshape(SLAB, -1), 'head', split_axis=0, concat_axis...  49.9 us
    all_to_all x4, waiting for transfers between devices, gathered(): lax.all_to_all(cells, 'head', split_axis=1, concat_axis=0, tiled=True)  37.2 us
    pallas_call x1, Pallas kernels, attention(): pl.pallas_call(functools.partial(attention_kernel, heads), out_shape=outs...  18.3 us
    ppermute x2, waiting for transfers between devices, with_rims(): lax.ppermute(cells, 'seq', [((i + 1) % count, i) for i in ring])  16.1 us
    all_to_all x4, starting transfers between devices, gathered(): lax.all_to_all(cells, 'head', split_axis=1, concat_axis=0, tiled=True)  16 us
    all_to_all x3, waiting for transfers between devices, returned(): lax.all_to_all(cells.reshape(SLAB, -1), 'head', split_axis=0, concat_axis...  14.1 us
    unnamed x23, local copies, waits for them, and re-layouts  12.5 us
    all_to_all x3, starting transfers between devices, returned(): lax.all_to_all(cells.reshape(SLAB, -1), 'head', split_axis=0, concat_axis...  12 us
  transfers between devices with their start and end apart: 13, of which 9 were waited for; matrix products, arithmetic and copies ran while one was open for 12% of the time, Pallas kernels for 0%

profile of v1, /device:TPU:225, one launch (start us, length us, event | category | flops | bytes accessed | tf_op | source)
XLA Modules:
  0.0 216.9 jit_solution(69714941280460737)
XLA Ops:
  0.6 1.6 copy.15
  3.4 5.1 %all-to-all-start.2 = ((bf16[128,8,384]{2,0,1:T(8,128)(2,1)}), bf16[128,8,384]{2,0,1:T(8,128)(2,1)S(1)}, u32[]{:S(2)}, u32[]{:S(2)}) async-start(bf16[128,8,384]{2,0,1:T(8,128)(2,1)} %copy.16), calls=%async_computation.2 | async-start | bytes 1572864 | tf_op jit(solution)/shard_map/all_to_all | solution.py:241
  8.9 1.2 copy.18
  10.1 10.1 %all-to-all-done.2 = bf16[128,8,384]{2,0,1:T(8,128)(2,1)S(1)} async-done(((bf16[128,8,384]{2,0,1:T(8,128)(2,1)}), bf16[128,8,384]{2,0,1:T(8,128)(2,1)S(1)}, u32[]{:S(2)}, u32[]{:S(2)}) %all-to-all-start.2) | async-done | bytes 786464 | tf_op jit(solution)/shard_map/all_to_all | solution.py:241
  20.2 3.8 %all-to-all-start.3 = ((bf16[128,8,384]{2,0,1:T(8,128)(2,1)}), bf16[128,8,384]{2,0,1:T(8,128)(2,1)S(1)}, u32[]{:S(2)}, u32[]{:S(2)}) async-start(bf16[128,8,384]{2,0,1:T(8,128)(2,1)} %copy.18), calls=%async_computation.3 | async-start | bytes 1572864 | tf_op jit(solution)/shard_map/all_to_all | solution.py:241
  24.4 1.2 copy.12
  25.5 9.6 %all-to-all-done.3 = bf16[128,8,384]{2,0,1:T(8,128)(2,1)S(1)} async-done(((bf16[128,8,384]{2,0,1:T(8,128)(2,1)}), bf16[128,8,384]{2,0,1:T(8,128)(2,1)S(1)}, u32[]{:S(2)}, u32[]{:S(2)}) %all-to-all-start.3) | async-done | bytes 786464 | tf_op jit(solution)/shard_map/all_to_all | solution.py:241
  35.2 3.5 %all-to-all-start = ((bf16[128,8,384]{2,0,1:T(8,128)(2,1)}), bf16[128,8,384]{2,0,1:T(8,128)(2,1)S(1)}, u32[]{:S(2)}, u32[]{:S(2)}) async-start(bf16[128,8,384]{2,0,1:T(8,128)(2,1)} %copy.12), calls=%async_computation | async-start | bytes 1572864 | tf_op jit(solution)/shard_map/all_to_all | solution.py:241
  38.7 2.9 %collective-permute-start.3 = (bf16[8,128,384]{2,1,0:T(8,128)(2,1)S(1)}, bf16[8,128,384]{2,1,0:T(8,128)(2,1)}, u32[]{:S(2)}, u32[]{:S(2)}) collective-permute-start(bf16[8,128,384]{2,1,0:T(8,128)(2,1)S(1)} %bitcast.23), channel_id=1, source_target_pairs={{1,0},{2,1},{3,2},{4,3},{5,4},{6,5},{7,6},{8,7},{9,8},{10,9},{11,1... | collective-permute-start | bytes 2359304 | tf_op jit(solution)/shard_map/ppermute | solution.py:233
  41.6 2.4 %collective-permute-start.2 = (bf16[8,128,384]{2,1,0:T(8,128)(2,1)S(1)}, bf16[8,128,384]{2,1,0:T(8,128)(2,1)}, u32[]{:S(2)}, u32[]{:S(2)}) collective-permute-start(bf16[8,128,384]{2,1,0:T(8,128)(2,1)S(1)} %bitcast.24), channel_id=1, source_target_pairs={{0,1},{1,2},{2,3},{3,4},{4,5},{5,6},{6,7},{7,8},{8,9},{9,10},{10,1... | collective-permute-start | bytes 2359304 | tf_op jit(solution)/shard_map/ppermute | solution.py:231
  44.0 3.2 %collective-permute-start = (bf16[8,128,384]{2,1,0:T(8,128)(2,1)S(1)}, bf16[8,128,384]{2,1,0:T(8,128)(2,1)}, u32[]{:S(2)}, u32[]{:S(2)}) collective-permute-start(bf16[8,128,384]{2,1,0:T(8,128)(2,1)S(1)} %bitcast.21), channel_id=1, source_target_pairs={{0,1},{1,2},{2,3},{3,4},{4,5},{5,6},{6,7},{7,8},{8,9},{9,10},{10,1... | collective-permute-start | bytes 2359304 | tf_op jit(solution)/shard_map/ppermute | solution.py:231
  47.2 1.5 copy.13
  49.9 15.5 %all-to-all-done = bf16[128,8,384]{2,0,1:T(8,128)(2,1)S(1)} async-done(((bf16[128,8,384]{2,0,1:T(8,128)(2,1)}), bf16[128,8,384]{2,0,1:T(8,128)(2,1)S(1)}, u32[]{:S(2)}, u32[]{:S(2)}) %all-to-all-start) | async-done | bytes 786464 | tf_op jit(solution)/shard_map/all_to_all | solution.py:241
  65.4 3.5 %all-to-all-start.1 = ((bf16[128,8,384]{2,0,1:T(8,128)(2,1)}), bf16[128,8,384]{2,0,1:T(8,128)(2,1)S(1)}, u32[]{:S(2)}, u32[]{:S(2)}) async-start(bf16[128,8,384]{2,0,1:T(8,128)(2,1)} %copy.14), calls=%async_computation.1 | async-start | bytes 1572864 | tf_op jit(solution)/shard_map/all_to_all | solution.py:241
  69.8 9.7 %collective-permute-done.3 = bf16[8,128,384]{2,1,0:T(8,128)(2,1)} collective-permute-done((bf16[8,128,384]{2,1,0:T(8,128)(2,1)S(1)}, bf16[8,128,384]{2,1,0:T(8,128)(2,1)}, u32[]{:S(2)}, u32[]{:S(2)}) %collective-permute-start.3) | collective-permute-done | bytes 786464 | tf_op jit(solution)/shard_map/ppermute | solution.py:233
  79.5 3.1 %pad_maximum_fusion.1.vp_hbm = bf16[24,128,384]{2,1,0:T(8,128)(2,1)} fusion(bf16[8,128,384]{2,1,0:T(8,128)(2,1)} %collective-permute-done.3, bf16[8,128,384]{2,1,0:T(8,128)(2,1)S(1)} %bitcast.25, bf16[8,128,384]{2,1,0:T(8,128)(2,1)} %collective-permute-done.2), kind=kLoop, calls=%fused_computation.2 | loop fusion | flops 2359296 | bytes 4718592 | tf_op jit(solution)/shard_map/concatenate | solution.py:229
  82.6 6.3 %collective-permute-done.1 = bf16[8,128,384]{2,1,0:T(8,128)(2,1)} collective-permute-done((bf16[8,128,384]{2,1,0:T(8,128)(2,1)S(1)}, bf16[8,128,384]{2,1,0:T(8,128)(2,1)}, u32[]{:S(2)}, u32[]{:S(2)}) %collective-permute-start.1) | collective-permute-done | bytes 786464 | tf_op jit(solution)/shard_map/ppermute | solution.py:233
  88.9 3.1 %pad_maximum_fusion.kp_hbm = bf16[24,128,384]{2,1,0:T(8,128)(2,1)} fusion(bf16[8,128,384]{2,1,0:T(8,128)(2,1)} %collective-permute-done.1, bf16[8,128,384]{2,1,0:T(8,128)(2,1)S(1)} %bitcast.22, bf16[8,128,384]{2,1,0:T(8,128)(2,1)} %collective-permute-done), kind=kLoop, calls=%fused_computation.1 | loop fusion | flops 2359296 | bytes 4718592 | tf_op jit(solution)/shard_map/concatenate | solution.py:229
  92.1 1.9 all-to-all-done.1
  94.9 18.3 %attention.1 = (bf16[8,128,384]{2,1,0:T(8,128)(2,1)}, bf16[8,128,384]{2,1,0:T(8,128)(2,1)}, bf16[2,8,128,384]{3,2,1,0:T(8,128)(2,1)}, bf16[2,8,128,384]{3,2,1,0:T(8,128)(2,1)}, f32[2,8,128,384]{3,2,1,0:T(8,128)}) custom-call(s32[256,12]{1,0:T(8,128)} %copy.19.list_hbm, s32[256]{0:T(256)} %count_ref.1, bf16[8,128,384]{2,1,0:T(8,128)(2,1)} %bitcast.36, ...), custom_call_target="tpu_custom_call" | custom-call | tf_op jit(solution)/shard_map/attention/pallas_call | solution.py:195
  113.2 10.2 %collective-permute-start.4 = (bf16[2,8,128,384]{3,2,1,0:T(8,128)(2,1)}, bf16[2,8,128,384]{3,2,1,0:T(8,128)(2,1)S(1)}, u32[]{:S(2)}, u32[]{:S(2)}) collective-permute-start(bf16[2,8,128,384]{3,2,1,0:T(8,128)(2,1)} %get-tuple-element.12), channel_id=1, source_target_pairs={{0,1},{1,2},{2,3},{3,4},{4,5},{5,6},{6,7},{7,8},{8,9},{9,10},{10,1... | collective-permute-start | bytes 4718600 | tf_op jit(solution)/shard_map/ppermute | solution.py:254
  123.4 49.9 %all_to_all.128 = bf16[8,128,384]{2,1,0:T(8,128)(2,1)} all-to-all(bf16[8,128,384]{2,1,0:T(8,128)(2,1)} %get-tuple-element.9), channel_id=1, replica_groups=mesh['head'=8,'seq'=32] {'head'}, dimensions={0} | all-to-all | bytes 1572864 | tf_op jit(solution)/shard_map/all_to_all | solution.py:245
  173.3 4.2 %all-to-all-start.5 = ((bf16[8,128,384]{2,1,0:T(8,128)(2,1)}), bf16[8,128,384]{2,1,0:T(8,128)(2,1)}, u32[]{:S(2)}, u32[]{:S(2)}) async-start(bf16[8,128,384]{2,1,0:T(8,128)(2,1)} %get-tuple-element.10), calls=%async_computation.5 | async-start | bytes 1572864 | tf_op jit(solution)/shard_map/all_to_all | solution.py:245
  178.7 1.2 copy-done.3
  179.9 3.4 %convert_add_fusion = f32[2,8,128,384]{3,2,1,0:T(8,128)S(1)} fusion(bf16[2,8,128,384]{3,2,1,0:T(8,128)(2,1)} %copy-done.3, f32[2,8,128,384]{3,2,1,0:T(8,128)} %get-tuple-element.11, bf16[2,8,128,384]{3,2,1,0:T(8,128)(2,1)} %copy-done.2), kind=kLoop, calls=%fused_computation | loop fusion | flops 3145728 | bytes 9437184 | tf_op jit(solution)/shard_map/add | solution.py:256
  184.3 5.3 %all-to-all-done.5 = bf16[8,128,384]{2,1,0:T(8,128)(2,1)} async-done(((bf16[8,128,384]{2,1,0:T(8,128)(2,1)}), bf16[8,128,384]{2,1,0:T(8,128)(2,1)}, u32[]{:S(2)}, u32[]{:S(2)}) %all-to-all-start.5) | async-done | bytes 786464 | tf_op jit(solution)/shard_map/all_to_all | solution.py:245
  189.6 4.2 %all-to-all-start.6 = ((bf16[8,128,384]{2,1,0:T(8,128)(2,1)}), bf16[8,128,384]{2,1,0:T(8,128)(2,1)}, u32[]{:S(2)}, u32[]{:S(2)}) async-start(bf16[8,128,384]{2,1,0:T(8,128)(2,1)} %fusion.1), calls=%async_computation.6 | async-start | bytes 1572864 | tf_op jit(solution)/shard_map/all_to_all | solution.py:245
  194.9 8.0 %all-to-all-done.6 = bf16[8,128,384]{2,1,0:T(8,128)(2,1)} async-done(((bf16[8,128,384]{2,1,0:T(8,128)(2,1)}), bf16[8,128,384]{2,1,0:T(8,128)(2,1)}, u32[]{:S(2)}, u32[]{:S(2)}) %all-to-all-start.6) | async-done | bytes 786464 | tf_op jit(solution)/shard_map/all_to_all | solution.py:245
  202.8 3.5 %all-to-all-start.7 = ((bf16[8,128,384]{2,1,0:T(8,128)(2,1)}), bf16[8,128,384]{2,1,0:T(8,128)(2,1)S(1)}, u32[]{:S(2)}, u32[]{:S(2)}) async-start(bf16[8,128,384]{2,1,0:T(8,128)(2,1)} %fusion.2), calls=%async_computation.7 | async-start | bytes 1572864 | tf_op jit(solution)/shard_map/all_to_all | solution.py:245
  206.4 1.5 copy.20
  209.1 1.5 copy.21
  211.7 1.5 copy.22
  (32 shorter events, 13.9 us)
Async XLA Ops:
  0.6 7.9 %copy-start.4 = (bf16[128,3072]{1,0:T(8,128)(2,1)S(1)}, bf16[128,3072]{1,0:T(8,128)(2,1)}, u32[]{:S(2)}) copy-start(bf16[128,3072]{1,0:T(8,128)(2,1)} %param.8) | copy-start | bytes 2359300
  3.4 16.8 %all-to-all-start.2 = ((bf16[128,8,384]{2,0,1:T(8,128)(2,1)}), bf16[128,8,384]{2,0,1:T(8,128)(2,1)S(1)}, u32[]{:S(2)}, u32[]{:S(2)}) async-start(bf16[128,8,384]{2,0,1:T(8,128)(2,1)} %copy.16), calls=%async_computation.2 | async-start | bytes 1572864 | tf_op jit(solution)/shard_map/all_to_all | solution.py:241
  8.5 15.5 %copy-start.5 = (bf16[128,3072]{1,0:T(8,128)(2,1)S(1)}, bf16[128,3072]{1,0:T(8,128)(2,1)}, u32[]{:S(2)}) copy-start(bf16[128,3072]{1,0:T(8,128)(2,1)} %param.6) | copy-start | bytes 2359300
  20.2 15.0 %all-to-all-start.3 = ((bf16[128,8,384]{2,0,1:T(8,128)(2,1)}), bf16[128,8,384]{2,0,1:T(8,128)(2,1)S(1)}, u32[]{:S(2)}, u32[]{:S(2)}) async-start(bf16[128,8,384]{2,0,1:T(8,128)(2,1)} %copy.18), calls=%async_computation.3 | async-start | bytes 1572864 | tf_op jit(solution)/shard_map/all_to_all | solution.py:241
  35.2 30.3 %all-to-all-start = ((bf16[128,8,384]{2,0,1:T(8,128)(2,1)}), bf16[128,8,384]{2,0,1:T(8,128)(2,1)S(1)}, u32[]{:S(2)}, u32[]{:S(2)}) async-start(bf16[128,8,384]{2,0,1:T(8,128)(2,1)} %copy.12), calls=%async_computation | async-start | bytes 1572864 | tf_op jit(solution)/shard_map/all_to_all | solution.py:241
  38.7 40.8 %collective-permute-start.3 = (bf16[8,128,384]{2,1,0:T(8,128)(2,1)S(1)}, bf16[8,128,384]{2,1,0:T(8,128)(2,1)}, u32[]{:S(2)}, u32[]{:S(2)}) collective-permute-start(bf16[8,128,384]{2,1,0:T(8,128)(2,1)S(1)} %bitcast.23), channel_id=1, source_target_pairs={{1,0},{2,1},{3,2},{4,3},{5,4},{6,5},{7,6},{8,7},{9,8},{10,9},{11,1... | collective-permute-start | bytes 2359304 | tf_op jit(solution)/shard_map/ppermute | solution.py:233
  41.6 37.9 %collective-permute-start.2 = (bf16[8,128,384]{2,1,0:T(8,128)(2,1)S(1)}, bf16[8,128,384]{2,1,0:T(8,128)(2,1)}, u32[]{:S(2)}, u32[]{:S(2)}) collective-permute-start(bf16[8,128,384]{2,1,0:T(8,128)(2,1)S(1)} %bitcast.24), channel_id=1, source_target_pairs={{0,1},{1,2},{2,3},{3,4},{4,5},{5,6},{6,7},{7,8},{8,9},{9,10},{10,1... | collective-permute-start | bytes 2359304 | tf_op jit(solution)/shard_map/ppermute | solution.py:231
  44.0 25.0 %copy-start.6 = (s32[256,12]{0,1:T(8,128)S(1)}, s32[256,12]{0,1:T(8,128)}, u32[]{:S(2)}) copy-start(s32[256,12]{0,1:T(8,128)} %param.10) | copy-start | bytes 36868
  44.0 45.0 %collective-permute-start.1 = (bf16[8,128,384]{2,1,0:T(8,128)(2,1)S(1)}, bf16[8,128,384]{2,1,0:T(8,128)(2,1)}, u32[]{:S(2)}, u32[]{:S(2)}) collective-permute-start(bf16[8,128,384]{2,1,0:T(8,128)(2,1)S(1)} %bitcast.20), channel_id=1, source_target_pairs={{1,0},{2,1},{3,2},{4,3},{5,4},{6,5},{7,6},{8,7},{9,8},{10,9},{11,1... | collective-permute-start | bytes 2359304 | tf_op jit(solution)/shard_map/ppermute | solution.py:233
  44.0 45.0 %collective-permute-start = (bf16[8,128,384]{2,1,0:T(8,128)(2,1)S(1)}, bf16[8,128,384]{2,1,0:T(8,128)(2,1)}, u32[]{:S(2)}, u32[]{:S(2)}) collective-permute-start(bf16[8,128,384]{2,1,0:T(8,128)(2,1)S(1)} %bitcast.21), channel_id=1, source_target_pairs={{0,1},{1,2},{2,3},{3,4},{4,5},{5,6},{6,7},{7,8},{8,9},{9,10},{10,1... | collective-permute-start | bytes 2359304 | tf_op jit(solution)/shard_map/ppermute | solution.py:231
  65.4 17.2 %copy-start = (bf16[128,8,384]{2,0,1:T(8,128)(2,1)}, bf16[128,8,384]{2,0,1:T(8,128)(2,1)S(1)}, u32[]{:S(2)}) copy-start(bf16[128,8,384]{2,0,1:T(8,128)(2,1)S(1)} %all-to-all-done) | copy-start | bytes 2359300
  65.4 28.5 %all-to-all-start.1 = ((bf16[128,8,384]{2,0,1:T(8,128)(2,1)}), bf16[128,8,384]{2,0,1:T(8,128)(2,1)S(1)}, u32[]{:S(2)}, u32[]{:S(2)}) async-start(bf16[128,8,384]{2,0,1:T(8,128)(2,1)} %copy.14), calls=%async_computation.1 | async-start | bytes 1572864 | tf_op jit(solution)/shard_map/all_to_all | solution.py:241
  94.0 0.9 copy-start.1
  113.2 64.3 %collective-permute-start.4 = (bf16[2,8,128,384]{3,2,1,0:T(8,128)(2,1)}, bf16[2,8,128,384]{3,2,1,0:T(8,128)(2,1)S(1)}, u32[]{:S(2)}, u32[]{:S(2)}) collective-permute-start(bf16[2,8,128,384]{3,2,1,0:T(8,128)(2,1)} %get-tuple-element.12), channel_id=1, source_target_pairs={{0,1},{1,2},{2,3},{3,4},{4,5},{5,6},{6,7},{7,8},{8,9},{9,10},{10,1... | collective-permute-start | bytes 4718600 | tf_op jit(solution)/shard_map/ppermute | solution.py:254
  123.4 54.1 %collective-permute-start.5 = (bf16[2,8,128,384]{3,2,1,0:T(8,128)(2,1)}, bf16[2,8,128,384]{3,2,1,0:T(8,128)(2,1)S(1)}, u32[]{:S(2)}, u32[]{:S(2)}) collective-permute-start(bf16[2,8,128,384]{3,2,1,0:T(8,128)(2,1)} %get-tuple-element.13), channel_id=1, source_target_pairs={{1,0},{2,1},{3,2},{4,3},{5,4},{6,5},{7,6},{8,7},{9,8},{10,9},{11,1... | collective-permute-start | bytes 4718600 | tf_op jit(solution)/shard_map/ppermute | solution.py:255
  173.3 16.3 %all-to-all-start.5 = ((bf16[8,128,384]{2,1,0:T(8,128)(2,1)}), bf16[8,128,384]{2,1,0:T(8,128)(2,1)}, u32[]{:S(2)}, u32[]{:S(2)}) async-start(bf16[8,128,384]{2,1,0:T(8,128)(2,1)} %get-tuple-element.10), calls=%async_computation.5 | async-start | bytes 1572864 | tf_op jit(solution)/shard_map/all_to_all | solution.py:245
  177.5 1.2 copy-start.2
  178.7 1.2 copy-start.3
  189.6 13.2 %all-to-all-start.6 = ((bf16[8,128,384]{2,1,0:T(8,128)(2,1)}), bf16[8,128,384]{2,1,0:T(8,128)(2,1)}, u32[]{:S(2)}, u32[]{:S(2)}) async-start(bf16[8,128,384]{2,1,0:T(8,128)(2,1)} %fusion.1), calls=%async_computation.6 | async-start | bytes 1572864 | tf_op jit(solution)/shard_map/all_to_all | solution.py:245
  202.8 12.5 %all-to-all-start.7 = ((bf16[8,128,384]{2,1,0:T(8,128)(2,1)}), bf16[8,128,384]{2,1,0:T(8,128)(2,1)S(1)}, u32[]{:S(2)}, u32[]{:S(2)}) async-start(bf16[8,128,384]{2,1,0:T(8,128)(2,1)} %fusion.2), calls=%async_computation.7 | async-start | bytes 1572864 | tf_op jit(solution)/shard_map/all_to_all | solution.py:245

commit v2 on v1

--- a/solution.py
+++ b/solution.py
@@ -30,7 +30,7 @@
         pltpu.make_async_copy(src, dst, in_sem.at[i])
         for i, (src, dst) in enumerate(
             [
-                (list_hbm.at[pl.ds(pl.multiple_of(slab * TILES_DEV, TILES_DEV), TILES_DEV)], list_ref),
+                (list_hbm, list_ref),
                 (kp_hbm, kp_ref),
                 (vp_hbm, vp_ref),
                 (q_hbm, q_ref),
@@ -69,7 +69,7 @@
             for u in range(GROUP):
                 j = c * GROUP + u
                 valid = j < used
-                slots.append(list_ref[a, jnp.where(valid, j, 0)] - (slab - 1) * TILES_DEV)
+                slots.append(list_ref[jnp.where(valid, j, 0), slab * TILES_DEV + a] - (slab - 1) * TILES_DEV)
                 extra.append(jnp.where(valid, 0.0, UNUSED).astype(jnp.float32))
             return slots, extra
 
@@ -165,9 +165,9 @@
         for h in range(heads):
             for kind in range(2):
                 part = slice((2 * h + 1 - kind) * HD, (2 * h + 2 - kind) * HD)
-                low_ref[kind, t, :, columns(h)] = acc_ref[t, :, part].astype(jnp.bfloat16)
-                up_ref[kind, t, :, columns(h)] = acc_ref[2 * TILES_DEV + t, :, part].astype(jnp.bfloat16)
-                own_ref[kind, t, :, columns(h)] = acc_ref[TILES_DEV + t, :, part]
+                low_ref[t, kind, :, columns(h)] = acc_ref[t, :, part].astype(jnp.bfloat16)
+                up_ref[t, kind, :, columns(h)] = acc_ref[2 * TILES_DEV + t, :, part].astype(jnp.bfloat16)
+                own_ref[t, kind, :, columns(h)] = acc_ref[TILES_DEV + t, :, part]
         return 0
 
     lax.fori_loop(0, TILES_DEV, finish, 0)
@@ -182,7 +182,7 @@
     heads = columns // HD
     own = (TILES_DEV, TILE, columns)
     pool = (3 * TILES_DEV, TILE, columns)
-    pair = (2,) + own
+    pair = (TILES_DEV, 2, TILE, columns)
     hbm = pl.BlockSpec(memory_space=pl.ANY)
     outs = (
         jax.ShapeDtypeStruct(own, jnp.bfloat16),
@@ -198,7 +198,7 @@
         in_specs=[hbm, pl.BlockSpec(memory_space=pltpu.SMEM), hbm, hbm, hbm, hbm],
         out_specs=(hbm,) * 5,
         scratch_shapes=[
-            pltpu.SMEM((TILES_DEV, LIST), jnp.int32),
+            pltpu.SMEM(tile_list.shape, jnp.int32),
             pltpu.VMEM(own, jnp.bfloat16),
             pltpu.VMEM(own, jnp.bfloat16),
             pltpu.VMEM(pool, jnp.bfloat16),
@@ -223,40 +223,285 @@
     )(tile_list, tile_count, query, cotangent, key_pool, value_pool)
 
 
-def with_rims(cells):
-    count = lax.axis_size("seq")
-    ring = range(count)
-    return jnp.concatenate(
-        [
-            lax.ppermute(cells, "seq", [(i, (i + 1) % count) for i in ring]),
-            cells,
-            lax.ppermute(cells, "seq", [((i + 1) % count, i) for i in ring]),
+MESH = pl.DeviceIdType.MESH
+
+
+def swapped(head, flag):
+    return head + flag * (1 - 2 * lax.rem(head, 2))
+
+
+def placement():
+    slabs = lax.axis_size("seq")
+    slab, head = lax.axis_index("seq"), lax.axis_index("head")
+    above, below = lax.rem(slab + 1, slabs), lax.rem(slab + slabs - 1, slabs)
+
+    def flag(s):
+        return lax.rem(lax.div(s, 2), 2)
+
+    own = flag(slab)
+    head_above = swapped(head, lax.rem(own + flag(above), 2))
+    head_below = swapped(head, lax.rem(own + flag(below), 2))
+    return slab, head, own, (above, head_above), (below, head_below)
+
+
+def entry_barrier(slab, head, heads, neighbours):
+    barrier = pltpu.get_barrier_semaphore()
+
+    def greet(r, _):
+        pl.semaphore_signal(
+            barrier, inc=1, device_id={"seq": slab, "head": lax.rem(head + r, heads)}, device_id_type=MESH
+        )
+        return 0
+
+    lax.fori_loop(1, heads, greet, 0)
+    for s, h in neighbours:
+        pl.semaphore_signal(barrier, inc=1, device_id={"seq": s, "head": h}, device_id_type=MESH)
+    pl.semaphore_wait(barrier, heads - 1 + len(neighbours))
+
+
+def gather_kernel(
+    k_hbm, v_hbm, q_hbm, g_hbm, kp_hbm, vp_hbm, qo_hbm, go_hbm,
+    local_sem, send_sem, recv_sem, rim_send, rim_recv,
+):
+    heads = lax.axis_size("head")
+    slab, head, flag, above, below = placement()
+    width = qo_hbm.shape[2]
+    entry_barrier(slab, head, heads, (above, below))
+    streams = [
+        (k_hbm, kp_hbm, TILES_DEV), (v_hbm, vp_hbm, TILES_DEV), (q_hbm, qo_hbm, 0), (g_hbm, go_hbm, 0)
+    ]
+
+    def block(i, peer):
+        group = swapped(peer, flag)
+        return streams[i][0].at[:, pl.ds(pl.multiple_of(group * width, width), width)]
+
+    def local(i):
+        _, dst, base = streams[i]
+        return pltpu.make_async_copy(block(i, head), dst.at[base + head], local_sem.at[i])
+
+    def exchange(i, peer, slot):
+        _, dst, base = streams[i]
+        return pltpu.make_async_remote_copy(
+            src_ref=block(i, peer),
+            dst_ref=dst.at[base + slot],
+            send_sem=send_sem.at[i, peer],
+            recv_sem=recv_sem.at[i, slot],
+            device_id={"seq": slab, "head": peer},
+            device_id_type=MESH,
+        )
+
+    def rim(i, side, tile):
+        dst = streams[i][1]
+        s, h = (above, below)[side]
+        return pltpu.make_async_remote_copy(
+            src_ref=dst.at[TILES_DEV + tile],
+            dst_ref=dst.at[2 * TILES_DEV * side + tile],
+            send_sem=rim_send.at[i, side, tile],
+            recv_sem=rim_recv.at[i, side, tile],
+            device_id={"seq": s, "head": h},
+            device_id_type=MESH,
+        )
+
+    def peers(body):
+        def step(r, _):
+            body(lax.rem(head + r, heads))
+            return 0
+
+        lax.fori_loop(1, heads, step, 0)
+
+    def send_all(i):
+        local(i).start()
+        peers(lambda peer: exchange(i, peer, head).start())
+
+    def forward(i):
+        local(i).wait()
+        rim(i, 0, head).start()
+        rim(i, 1, head).start()
+
+        def arrived(peer):
+            exchange(i, peer, peer).wait_recv()
+            rim(i, 0, peer).start()
+            rim(i, 1, peer).start()
+
+        peers(arrived)
+
+    send_all(0)
+    send_all(1)
+    forward(0)
+    send_all(2)
+    forward(1)
+    send_all(3)
+    for i in (2, 3):
+        local(i).wait()
+        peers(lambda peer: exchange(i, peer, peer).wait_recv())
+    for i in range(4):
+        peers(lambda peer: exchange(i, peer, head).wait_send())
+
+    def settle(tile, _):
+        for i in range(2):
+            for side in range(2):
+                rim(i, side, tile).wait_recv()
+                rim(i, side, tile).wait_send()
+        return 0
+
+    lax.fori_loop(0, TILES_DEV, settle, 0)
+
+
+def gather(key, value, query, cotangent):
+    columns = key.shape[1] // TILES_DEV
+    hbm = pl.BlockSpec(memory_space=pl.ANY)
+    own = jax.ShapeDtypeStruct((TILES_DEV, TILE, columns), jnp.bfloat16)
+    pool = jax.ShapeDtypeStruct((3 * TILES_DEV, TILE, columns), jnp.bfloat16)
+    return pl.pallas_call(
+        gather_kernel,
+        out_shape=(pool, pool, own, own),
+        in_specs=[hbm] * 4,
+        out_specs=(hbm,) * 4,
+        scratch_shapes=[
+            pltpu.SemaphoreType.DMA((4,)),
+            pltpu.SemaphoreType.DMA((4, TILES_DEV)),
+            pltpu.SemaphoreType.DMA((4, TILES_DEV)),
+            pltpu.SemaphoreType.DMA((2, 2, TILES_DEV)),
+            pltpu.SemaphoreType.DMA((2, 2, TILES_DEV)),
         ],
-        axis=0,
-    )
+        compiler_params=pltpu.CompilerParams(collective_id=0, has_side_effects=True),
+        name="gather",
+    )(key, value, query, cotangent)
+
+
+def scatter_kernel(
+    o_hbm, dq_hbm, low_hbm, up_hbm, own_hbm, oo_hbm, dqo_hbm, dko_hbm, dvo_hbm,
+    own_ref, from_below, from_above, dk_ref, dv_ref,
+    own_sem, local_sem, send_sem, recv_sem, rim_send, rim_recv,
+):
+    heads = lax.axis_size("head")
+    slab, head, flag, above, below = placement()
+    width = o_hbm.shape[2]
+    columns = pl.ds(pl.multiple_of(swapped(head, flag) * width, width), width)
+    own_load = pltpu.make_async_copy(own_hbm, own_ref, own_sem)
+    own_load.start()
+    entry_barrier(slab, head, heads, (above, below))
+
+    def rim(side, tile):
+        s, h = (above, below)[side]
+        return pltpu.make_async_remote_copy(
+            src_ref=(up_hbm, low_hbm)[side].at[tile],
+            dst_ref=(from_below, from_above)[side].at[tile],
+            send_sem=rim_send.at[side, tile],
+            recv_sem=rim_recv.at[side, tile],
+            device_id={"seq": s, "head": h},
+            device_id_type=MESH,
+        )
+
+    streams = [(o_hbm, oo_hbm), (dq_hbm, dqo_hbm), (dk_ref, dko_hbm), (dv_ref, dvo_hbm)]
+
+    def local(i):
+        src, dst = streams[i]
+        return pltpu.make_async_copy(src.at[head], dst.at[:, columns], local_sem.at[i])
+
+    def exchange(i, peer, slot):
+        src, dst = streams[i]
+        return pltpu.make_async_remote_copy(
+            src_ref=src.at[peer],
+            dst_ref=dst.at[:, columns],
+            send_sem=send_sem.at[i, peer],
+            recv_sem=recv_sem.at[i, slot],
+            device_id={"seq": slab, "head": peer},
+            device_id_type=MESH,
+        )
+
+    def peers(body):
+        def step(r, _):
+            body(lax.rem(head + r, heads))
+            return 0
+
+        lax.fori_loop(1, heads, step, 0)
+
+    def start_rims(r, _):
+        for side, (_, h) in enumerate((above, below)):
+            rim(side, lax.rem(h + r, heads)).start()
+        return 0
+
+    lax.fori_loop(1, heads + 1, start_rims, 0)
+    for i in range(2):
+        peers(lambda peer: exchange(i, peer, head).start())
+        local(i).start()
+    own_load.wait()
+
+    def summed(tile):
+        rim(0, tile).wait_recv()
+        rim(1, tile).wait_recv()
+        for kind, (ref, factor) in enumerate(((dk_ref, SCALING), (dv_ref, None))):
+            total = (
+                own_ref[tile, kind]
+                + from_below[tile, kind].astype(jnp.float32)
+                + from_above[tile, kind].astype(jnp.float32)
+            )
+            if factor is not None:
+                total = factor * total
+            ref[tile] = total.astype(jnp.bfloat16)
+
+    def finish(peer):
+        summed(peer)
+        exchange(2, peer, head).start()
+        exchange(3, peer, head).start()
+
+    peers(finish)
+    summed(head)
+    local(2).start()
+    local(3).start()
+
+    def settle(peer):
+        for i in range(4):
+            exchange(i, peer, peer).wait_recv()
+            exchange(i, peer, head).wait_send()
+
+    peers(settle)
+    for i in range(4):
+        local(i).wait()
+
+    def settle_rims(tile, _):
+        rim(0, tile).wait_send()
+        rim(1, tile).wait_send()
+        return 0
+
+    lax.fori_loop(0, TILES_DEV, settle_rims, 0)
+
+
+def scatter(out, dq, low, up, own):
+    width = out.shape[2]
+    hbm = pl.BlockSpec(memory_space=pl.ANY)
+    tokens = jax.ShapeDtypeStruct((TILE, TILES_DEV * width), jnp.bfloat16)
+    rims = (TILES_DEV, 2, TILE, width)
+    return pl.pallas_call(
+        scatter_kernel,
+        out_shape=(tokens,) * 4,
+        in_specs=[hbm] * 5,
+        out_specs=(hbm,) * 4,
+        scratch_shapes=[
+            pltpu.VMEM(rims, jnp.float32),
+            pltpu.VMEM(rims, jnp.bfloat16),
+            pltpu.VMEM(rims, jnp.bfloat16),
+            pltpu.VMEM((TILES_DEV, TILE, width), jnp.bfloat16),
+            pltpu.VMEM((TILES_DEV, TILE, width), jnp.bfloat16),
+            pltpu.SemaphoreType.DMA(()),
+            pltpu.SemaphoreType.DMA((4,)),
+            pltpu.SemaphoreType.DMA((4, TILES_DEV)),
+            pltpu.SemaphoreType.DMA((4, TILES_DEV)),
+            pltpu.SemaphoreType.DMA((2, TILES_DEV)),
+            pltpu.SemaphoreType.DMA((2, TILES_DEV)),
+        ],
+        compiler_params=pltpu.CompilerParams(
+            collective_id=1, has_side_effects=True, vmem_limit_bytes=32 * 2**20
+        ),
+        name="scatter",
+    )(out, dq, low, up, own)
 
 
 def per_device(query, key, value, grad_out, tile_list, tile_count):
-    def gathered(cells):
-        moved = lax.all_to_all(cells, "head", split_axis=1, concat_axis=0, tiled=True)
-        return moved.reshape(TILES_DEV, TILE, moved.shape[1])
-
-    def returned(cells):
-        return lax.all_to_all(cells.reshape(SLAB, -1), "head", split_axis=0, concat_axis=1, tiled=True)
-
-    key_pool = with_rims(gathered(key))
-    value_pool = with_rims(gathered(value))
-    out, dq, low, up, own = attention(
-        tile_list, tile_count, gathered(query), gathered(grad_out), key_pool, value_pool
-    )
-    count = lax.axis_size("seq")
-    ring = range(count)
-    from_below = lax.ppermute(up, "seq", [(i, (i + 1) % count) for i in ring])
-    from_above = lax.ppermute(low, "seq", [((i + 1) % count, i) for i in ring])
-    total = own + from_below.astype(jnp.float32) + from_above.astype(jnp.float32)
-    dk = (SCALING * total[0]).astype(jnp.bfloat16)
-    dv = total[1].astype(jnp.bfloat16)
-    return returned(out), returned(dq), returned(dk), returned(dv)
+    key_pool, value_pool, queries, cotangents = gather(key, value, query, grad_out)
+    parts = attention(tile_list.T, tile_count, queries, cotangents, key_pool, value_pool)
+    return tuple(scatter(*parts))
 
 
 def solution(mesh):

time: 218 us -> 139 us (0.64)
  the two profiles are of different devices: /device:TPU:225 before, /device:TPU:1 now
where the time goes in v2:
time: 139 us; the launch traced here: 137 us
  Pallas kernels  126 us (91%)
  local copies, waits for them, and re-layouts  10.5 us (8%)
    pallas_call x1, Pallas kernels, gather(): pl.pallas_call(gather_kernel, out_shape=(pool, pool, own, own), in_specs=...  53.6 us
    pallas_call x1, Pallas kernels, scatter(): pl.pallas_call(scatter_kernel, out_shape=(tokens,) * 4, in_specs=[hbm] *...  38.2 us
    pallas_call x1, Pallas kernels, attention(): pl.pallas_call(functools.partial(attention_kernel, heads), out_shape=outs...  33.8 us
    unnamed x14, local copies, waits for them, and re-layouts  10.5 us

profile of v2, /device:TPU:1, one launch (start us, length us, event | category | flops | bytes accessed | tf_op | source)
XLA Modules:
  0.0 136.8 jit_solution(1116289191943081261)
XLA Ops:
  0.6 53.6 %gather.1 = (bf16[24,128,384]{2,1,0:T(8,128)(2,1)}, bf16[24,128,384]{2,1,0:T(8,128)(2,1)}, bf16[8,128,384]{2,1,0:T(8,128)(2,1)}, bf16[8,128,384]{2,1,0:T(8,128)(2,1)}) custom-call(bf16[128,3072]{1,0:T(8,128)(2,1)} %k_hbm.1, bf16[128,3072]{1,0:T(8,128)(2,1)} %v_hbm.1, bf16[128,3072]{1,0:T(8,128)(2,1)} %q_hbm.1, bf16[128,3072]{1,0:T(8,128)(2,1)} %g_hbm.1), custom_call_target="tpu_custom_call" | custom-call | tf_op jit(solution)/shard_map/gather/pallas_call | solution.py:355
  54.3 33.8 %attention.1 = (bf16[8,128,384]{2,1,0:T(8,128)(2,1)}, bf16[8,128,384]{2,1,0:T(8,128)(2,1)}, bf16[8,2,128,384]{3,2,1,0:T(8,128)(2,1)}, bf16[8,2,128,384]{3,2,1,0:T(8,128)(2,1)}, f32[8,2,128,384]{3,2,1,0:T(8,128)}) custom-call(s32[12,256]{1,0:T(8,128)} %bitcast.1, s32[256]{0:T(256)} %count_ref.1, bf16[8,128,384]{2,1,0:T(8,128)(2,1)} %get-tuple-element.13.q_hbm, ...), custom_call_target="tpu_custom_call" | custom-call | tf_op jit(solution)/shard_map/attention/pallas_call | solution.py:195
  88.0 0.0 copy-start
  88.0 1.9 %copy-done = f32[8,2,128,384]{3,2,1,0:T(8,128)S(1)} copy-done((f32[8,2,128,384]{3,2,1,0:T(8,128)S(1)}, f32[8,2,128,384]{3,2,1,0:T(8,128)}, u32[]{:S(2)}) %copy-start) | copy-done | bytes 3145752
  89.9 0.0 copy-start.1
  89.9 1.4 %copy-done.1 = bf16[8,2,128,384]{3,2,1,0:T(8,128)(2,1)S(1)} copy-done((bf16[8,2,128,384]{3,2,1,0:T(8,128)(2,1)S(1)}, bf16[8,2,128,384]{3,2,1,0:T(8,128)(2,1)}, u32[]{:S(2)}) %copy-start.1) | copy-done | bytes 1572888
  91.3 0.0 copy-start.2
  91.3 1.4 %copy-done.2 = bf16[8,2,128,384]{3,2,1,0:T(8,128)(2,1)S(1)} copy-done((bf16[8,2,128,384]{3,2,1,0:T(8,128)(2,1)S(1)}, bf16[8,2,128,384]{3,2,1,0:T(8,128)(2,1)}, u32[]{:S(2)}) %copy-start.2) | copy-done | bytes 1572888
  92.7 0.0 copy-start.3
  92.7 1.1 copy-done.3
  93.9 0.0 copy-start.4
  93.9 1.1 copy-done.4
  95.0 38.2 %scatter.1 = (bf16[128,3072]{1,0:T(8,128)(2,1)S(1)}, bf16[128,3072]{1,0:T(8,128)(2,1)S(1)}, bf16[128,3072]{1,0:T(8,128)(2,1)S(1)}, bf16[128,3072]{1,0:T(8,128)(2,1)S(1)}) custom-call(bf16[8,128,384]{2,1,0:T(8,128)(2,1)S(1)} %copy-done.3, bf16[8,128,384]{2,1,0:T(8,128)(2,1)S(1)} %copy-done.4, bf16[8,2,128,384]{3,2,1,0:T(8,128)(2,1)S(1)} %copy-done.1, ...), custom_call_target="tpu_custom_call" | custom-call | tf_op jit(solution)/shard_map/scatter/pallas_call | solution.py:476
  133.2 0.9 copy.14
  134.1 0.9 copy.15
  135.0 0.9 copy.16
  135.9 0.9 copy.17
Async XLA Ops:
  88.0 1.9 %copy-start = (f32[8,2,128,384]{3,2,1,0:T(8,128)S(1)}, f32[8,2,128,384]{3,2,1,0:T(8,128)}, u32[]{:S(2)}) copy-start(f32[8,2,128,384]{3,2,1,0:T(8,128)} %get-tuple-element.21.own_hbm) | copy-start | bytes 9437188
  89.9 1.4 %copy-start.1 = (bf16[8,2,128,384]{3,2,1,0:T(8,128)(2,1)S(1)}, bf16[8,2,128,384]{3,2,1,0:T(8,128)(2,1)}, u32[]{:S(2)}) copy-start(bf16[8,2,128,384]{3,2,1,0:T(8,128)(2,1)} %get-tuple-element.19.low_hbm) | copy-start | bytes 4718596
  91.3 1.4 %copy-start.2 = (bf16[8,2,128,384]{3,2,1,0:T(8,128)(2,1)S(1)}, bf16[8,2,128,384]{3,2,1,0:T(8,128)(2,1)}, u32[]{:S(2)}) copy-start(bf16[8,2,128,384]{3,2,1,0:T(8,128)(2,1)} %get-tuple-element.20.up_hbm) | copy-start | bytes 4718596
  92.7 1.1 copy-start.3
  93.9 1.1 copy-start.4

commit v3 on v0

v3 whole, which is shorter than its diff:
```python
import functools

import jax
import jax.numpy as jnp
from jax import lax
from jax.experimental import pallas as pl
from jax.experimental.pallas import tpu as pltpu
from jax.sharding import PartitionSpec as P

HD = 128
TILE = 128
TILES_DEV = 8
FRAMES = 3
POOL = FRAMES * TILES_DEV
LIST = 12
SCALING = HD ** (-0.5)
LOG2E = 1.4426950408889634
UNUSED = 1e30
MESH = pl.DeviceIdType.MESH


def swapped(head, flag):
    return head + flag * (1 - 2 * lax.rem(head, 2))


def placement():
    slabs = lax.axis_size("seq")
    slab, head = lax.axis_index("seq"), lax.axis_index("head")
    above, below = lax.rem(slab + 1, slabs), lax.rem(slab + slabs - 1, slabs)

    def flag(s):
        return lax.rem(lax.div(s, 2), 2)

    own = flag(slab)
    head_above = swapped(head, lax.rem(own + flag(above), 2))
    head_below = swapped(head, lax.rem(own + flag(below), 2))
    return slab, head, own, (above, head_above), (below, head_below)


def entry_barrier(slab, head, devices, neighbours):
    barrier = pltpu.get_barrier_semaphore()

    def greet(r, _):
        pl.semaphore_signal(
            barrier, inc=1, device_id={"seq": slab, "head": lax.rem(head + r, devices)}, device_id_type=MESH
        )
        return 0

    lax.fori_loop(1, devices, greet, 0)
    for s, h in neighbours:
        pl.semaphore_signal(barrier, inc=1, device_id={"seq": s, "head": h}, device_id_type=MESH)
    pl.semaphore_wait(barrier, devices - 1 + len(neighbours))


def folded(op, rows):
    return functools.reduce(op, [rows[r : r + 8] for r in range(0, rows.shape[0], 8)])


def fused_kernel(
    heads,
    list_ref, count_ref, k_hbm, v_hbm, q_hbm, g_hbm,
    o_out, dq_out, dk_out, dv_out,
    kv_ref, q_ref, g_ref, acc_ref, mask_ref, w_ref, e_ref, dp_ref, stat_ref, ot_ref, dqt_ref,
    o_ref, dq_ref, dk_ref, dv_ref, low_ref, up_ref, from_below, from_above,
    local_sem, kv_recv, qg_recv, in_send, rim_recv, rim_send,
    out_local, out_send, out_recv, part_recv, part_send,
):
    devices = lax.axis_size("head")
    slab, head, flag, above, below = placement()
    sources = (v_hbm, k_hbm, q_hbm, g_hbm)
    results = ((o_ref, o_out), (dq_ref, dq_out), (dk_ref, dk_out), (dv_ref, dv_out))

    def columns(group, i):
        return pl.ds(pl.multiple_of((group * heads + i) * HD, HD), HD)

    def landing(x, i, slot):
        return kv_ref.at[i, TILES_DEV + slot, x] if x < 2 else (q_ref, g_ref)[x - 2].at[i, slot]

    def local(x, i):
        return pltpu.make_async_copy(
            sources[x].at[:, columns(swapped(head, flag), i)], landing(x, i, head), local_sem.at[i, x]
        )

    def incoming(x, i, peer, slot):
        return pltpu.make_async_remote_copy(
            src_ref=sources[x].at[:, columns(swapped(peer, flag), i)],
            dst_ref=landing(x, i, slot),
            send_sem=in_send.at[i, x],
            recv_sem=kv_recv.at[i, x, slot] if x < 2 else qg_recv.at[i, x - 2],
            device_id={"seq": slab, "head": peer},
            device_id_type=MESH,
        )

    def whole(ref, send_sem, recv_sem):
        return pltpu.make_async_remote_copy(
            src_ref=ref, dst_ref=ref, send_sem=send_sem, recv_sem=recv_sem,
            device_id={"seq": above[0], "head": above[1]}, device_id_type=MESH,
        )

    def rim(i, side, tile):
        s, h = (above, below)[side]
        return pltpu.make_async_remote_copy(
            src_ref=kv_ref.at[i, TILES_DEV + tile],
            dst_ref=kv_ref.at[i, 2 * TILES_DEV * side + tile],
            send_sem=rim_send.at[i, side],
            recv_sem=rim_recv.at[i, side],
            device_id={"seq": s, "head": h},
            device_id_type=MESH,
        )

    def part(i, side, tile):
        s, h = (above, below)[side]
        return pltpu.make_async_remote_copy(
            src_ref=(up_ref, low_ref)[side].at[i, tile],
            dst_ref=(from_below, from_above)[side].at[i, tile],
            send_sem=part_send.at[i, side],
            recv_sem=part_recv.at[i, side, tile],
            device_id={"seq": s, "head": h},
            device_id_type=MESH,
        )

    def result_local(x, i):
        src, dst = results[x]
        return pltpu.make_async_copy(
            src.at[i, head], dst.at[:, columns(swapped(head, flag), i)], out_local.at[i, x]
        )

    def result(x, i, peer):
        src, dst = results[x]
        return pltpu.make_async_remote_copy(
            src_ref=src.at[i, peer],
            dst_ref=dst.at[:, columns(swapped(head, flag), i)],
            send_sem=out_send.at[i, x],
            recv_sem=out_recv.at[i, x],
            device_id={"seq": slab, "head": peer},
            device_id_type=MESH,
        )

    def peers(body):
        def step(r, _):
            body(lax.rem(head + r, devices))
            return 0

        lax.fori_loop(1, devices, step, 0)

    def send(i, streams):
        def both(peer):
            for x in streams:
                incoming(x, i, peer, head).start()

        peers(both)

    def forward(i, r):
        tile = lax.rem(head + r, devices)

        @pl.when(r == 0)
        def _():
            local(0, i).wait()
            local(1, i).wait()

        @pl.when(r > 0)
        def _():
            incoming(0, i, tile, tile).wait_recv()
            incoming(1, i, tile, tile).wait_recv()

        rim(i, 0, tile).start()
        rim(i, 1, tile).start()

    def finish(i, r):
        tile = lax.rem(head + r, devices)
        part(i, 0, tile).wait_recv()
        part(i, 1, tile).wait_recv()
        dv = acc_ref[i, TILES_DEV + tile, :, :HD] + (
            from_below[i, tile, 0].astype(jnp.float32) + from_above[i, tile, 0].astype(jnp.float32)
        )
        dk = acc_ref[i, TILES_DEV + tile, :, HD:] + (
            from_below[i, tile, 1].astype(jnp.float32) + from_above[i, tile, 1].astype(jnp.float32)
        )
        dk_ref[i, tile] = (SCALING * dk).astype(jnp.bfloat16)
        dv_ref[i, tile] = dv.astype(jnp.bfloat16)

        @pl.when(r > 0)
        def _():
            result(2, i, tile).start()
            result(3, i, tile).start()

        @pl.when(r == 0)
        def _():
            result_local(2, i).start()
            result_local(3, i).start()

    def service(i, r):
        @pl.when(i < heads - 1)
        def _():
            forward(i + 1, r)

        @pl.when(i == heads - 1)
        def _():
            finish(0, r)

    def attend(i, a, start, count):
        rows = count * TILE
        w_ref[:TILE, :HD] = g_ref[i, a]
        w_ref[TILE:, HD:] = q_ref[i, a]

        def pairs(f):
            first = f * TILES_DEV + start
            values = kv_ref[i, pl.ds(first, count), 0].reshape(rows, HD)
            keys = kv_ref[i, pl.ds(first, count), 1].reshape(rows, HD)
            return first, values, keys

        def scores(f, _):
            first, values, keys = pairs(f)
            both = lax.dot_general(
                jnp.concatenate([values, keys], axis=1), w_ref[...], (((1,), (1,)), ((), ())),
                preferred_element_type=jnp.float32,
            )
            grad_prob = both[:, :TILE]
            score = both[:, TILE:]
            extra = [mask_ref[a * POOL + first + u] for u in range(count)]
            top = functools.reduce(
                jnp.maximum,
                [folded(jnp.maximum, score[u * TILE : (u + 1) * TILE]) - extra[u] for u in range(count)],
            )
            top = jnp.maximum(jnp.max(top, axis=0, keepdims=True), -0.1 * UNUSED)
            total = jnp.zeros((8, TILE), jnp.float32)
            dots = jnp.zeros((8, TILE), jnp.float32)
            for u in range(count):
                at = slice(u * TILE, (u + 1) * TILE)
                e = jnp.exp2((score[at] - (top + extra[u])) * (SCALING * LOG2E))
                e_ref[f, at] = e
                total = total + folded(jnp.add, e)
                dots = dots + folded(jnp.add, e * grad_prob[at])
            dp_ref[f, :rows] = grad_prob
            stat_ref[f, 0:1] = top
            stat_ref[f, 1:2] = jnp.sum(total, axis=0, keepdims=True)
            stat_ref[f, 2:3] = jnp.sum(dots, axis=0, keepdims=True)
            return 0

        lax.fori_loop(0, FRAMES, scores, 0)

        top = functools.reduce(jnp.maximum, [stat_ref[f, 0:1] for f in range(FRAMES)])
        weights = [jnp.exp2((stat_ref[f, 0:1] - top) * (SCALING * LOG2E)) for f in range(FRAMES)]
        total = sum(weights[f] * stat_ref[f, 1:2] for f in range(FRAMES))
        dots = sum(weights[f] * stat_ref[f, 2:3] for f in range(FRAMES))
        inverse = 1.0 / total
        for f in range(FRAMES):
            stat_ref[f, 3:4] = weights[f] * inverse
            stat_ref[f, 4:5] = dots * inverse
        ot_ref[...] = jnp.zeros_like(ot_ref)
        dqt_ref[...] = jnp.zeros_like(dqt_ref)

        def grads(f, _):
            first, values, keys = pairs(f)
            p = e_ref[f, :rows] * stat_ref[f, 3:4]
            ds = (p * (dp_ref[f, :rows] - stat_ref[f, 4:5])).astype(jnp.bfloat16)
            pb = p.astype(jnp.bfloat16)
            both = lax.dot_general(
                jnp.concatenate([pb, ds], axis=1), w_ref[...], (((1,), (0,)), ((), ())),
                preferred_element_type=jnp.float32,
            )
            for u in range(count):
                acc_ref[i, first + u] += both[u * TILE : (u + 1) * TILE]
            ot_ref[...] += lax.dot_general(
                values, pb, (((0,), (0,)), ((), ())), preferred_element_type=jnp.float32
            )
            dqt_ref[...] += lax.dot_general(
                keys, ds, (((0,), (0,)), ((), ())), preferred_element_type=jnp.float32
            )
            return 0

        lax.fori_loop(0, FRAMES, grads, 0)
        o_ref[i, a] = ot_ref[...].T.astype(jnp.bfloat16)
        dq_ref[i, a] = (dqt_ref[...].T * SCALING).astype(jnp.bfloat16)

    for i in range(heads):
        for x in range(4):
            local(x, i).start()
    entry_barrier(slab, head, devices, (above, below))
    send(0, (0, 1))
    forward(0, 0)
    send(0, (2, 3))

    def masks(a, _):
        used = count_ref[slab * TILES_DEV + a]
        listed = [
            jnp.where(j < used, list_ref[j, slab * TILES_DEV + a] - (slab - 1) * TILES_DEV, -1)
            for j in range(LIST)
        ]

        def one(slot, _):
            hit = functools.reduce(jnp.logical_or, [entry == slot for entry in listed])
            mask_ref[a * POOL + slot] = jnp.where(hit, 0.0, UNUSED).astype(jnp.float32)
            return 0

        lax.fori_loop(0, POOL, one, 0)
        return 0

    lax.fori_loop(0, TILES_DEV, masks, 0)
    w_ref[...] = jnp.zeros_like(w_ref)

    def first_tiles(r, _):
        forward(0, r)
        return 0

    lax.fori_loop(1, devices, first_tiles, 0)
    send(1, (0, 1))

    others = pl.ds(0, devices - 1)

    def head_step(i, _):
        def clear(slot, _):
            acc_ref[i, slot] = jnp.zeros((TILE, 2 * HD), jnp.float32)
            return 0

        lax.fori_loop(0, POOL, clear, 0)

        @pl.when(i < heads - 1)
        def _():
            send(i + 1, (2, 3))

        @pl.when(i < heads - 2)
        def _():
            send(i + 2, (0, 1))

        for x in (2, 3):
            local(x, i).wait()
            whole(q_ref.at[i, others], in_send.at[i, x], qg_recv.at[i, x - 2]).wait_recv()
        for side in range(2):
            whole(
                kv_ref.at[i, pl.ds(TILES_DEV, TILES_DEV)], rim_send.at[i, side], rim_recv.at[i, side]
            ).wait_recv()

        def outer(n, _):
            half = lax.div(n, 2)
            attend(i, n + 4 * half, 4 * half, 4)
            service(i, n)
            return 0

        def inner(n, _):
            attend(i, n + 2, 2 * lax.div(n, 2), 6)
            service(i, n + 4)
            return 0

        lax.fori_loop(0, 4, outer, 0)
        lax.fori_loop(0, 4, inner, 0)

        def leave(r, _):
            for side, (ref, (_, h)) in enumerate(((up_ref, above), (low_ref, below))):
                tile = lax.rem(h + 1 + r, devices)
                for kind in range(2):
                    ref[i, tile, kind] = acc_ref[
                        i, 2 * TILES_DEV * (1 - side) + tile, :, kind * HD : (kind + 1) * HD
                    ].astype(jnp.bfloat16)
                part(i, side, tile).start()
            return 0

        lax.fori_loop(0, devices, leave, 0)

        def both(peer):
            result(0, i, peer).start()
            result(1, i, peer).start()

        peers(both)
        result_local(0, i).start()
        result_local(1, i).start()
        return 0

    lax.fori_loop(0, heads, head_step, 0)

    def last(n, _):
        i = 1 + lax.div(n, devices)
        finish(i, lax.rem(n + 1, devices))
        return 0

    lax.fori_loop(0, (heads - 1) * devices, last, 0)

    def settle(i, _):
        for x in range(4):
            result_local(x, i).wait()
            whole(q_ref.at[i, others], out_send.at[i, x], out_recv.at[i, x]).wait()
            whole(q_ref.at[i, others], in_send.at[i, x], out_recv.at[i, x]).wait_send()
        for side in range(2):
            whole(
                kv_ref.at[i, pl.ds(TILES_DEV, TILES_DEV)], rim_send.at[i, side], rim_recv.at[i, side]
            ).wait_send()
            whole(low_ref.at[i], part_send.at[i, side], part_recv.at[i, side, 0]).wait_send()
        return 0

    lax.fori_loop(0, heads, settle, 0)


def fused(tile_list, tile_count, key, value, query, cotangent):
    heads = key.shape[1] // (TILES_DEV * HD)
    hbm = pl.BlockSpec(memory_space=pl.ANY)
    smem = pl.BlockSpec(memory_space=pltpu.SMEM)
    tokens = jax.ShapeDtypeStruct(key.shape, jnp.bfloat16)
    tiles = pltpu.VMEM((heads, TILES_DEV, TILE, HD), jnp.bfloat16)
    pairs = pltpu.VMEM((heads, TILES_DEV, 2, TILE, HD), jnp.bfloat16)
    dma = pltpu.SemaphoreType.DMA
    return pl.pallas_call(
        functools.partial(fused_kernel, heads),
        out_shape=(tokens,) * 4,
        in_specs=[smem, smem, hbm, hbm, hbm, hbm],
        out_specs=(hbm,) * 4,
        scratch_shapes=[
            pltpu.VMEM((heads, POOL, 2, TILE, HD), jnp.bfloat16),
            tiles,
            tiles,
            pltpu.VMEM((heads, POOL, TILE, 2 * HD), jnp.float32),
            pltpu.SMEM((TILES_DEV * POOL,), jnp.float32),
            pltpu.VMEM((2 * TILE, 2 * HD), jnp.bfloat16),
            pltpu.VMEM((FRAMES, 6 * TILE, TILE), jnp.float32),
            pltpu.VMEM((FRAMES, 6 * TILE, TILE), jnp.float32),
            pltpu.VMEM((FRAMES, 8, TILE), jnp.float32),
            pltpu.VMEM((HD, TILE), jnp.float32),
            pltpu.VMEM((HD, TILE), jnp.float32),
            tiles,
            tiles,
            tiles,
            tiles,
            pairs,
            pairs,
            pairs,
            pairs,
            dma((heads, 4)),
            dma((heads, 2, TILES_DEV)),
            dma((heads, 2)),
            dma((heads, 4)),
            dma((heads, 2)),
            dma((heads, 2)),
            dma((heads, 4)),
            dma((heads, 4)),
            dma((heads, 4)),
            dma((heads, 2, TILES_DEV)),
            dma((heads, 2)),
        ],
        compiler_params=pltpu.CompilerParams(
            collective_id=0, has_side_effects=True, vmem_limit_bytes=58 * 2**20
        ),
        name="fused",
    )(tile_list, tile_count, key, value, query, cotangent)


def per_device(query, key, value, grad_out, tile_list, tile_count):
    return tuple(fused(tile_list.T, tile_count, key, value, query, grad_out))


def solution(mesh):
    tokens = P(("seq", "head"), None)
    return jax.shard_map(
        per_device,
        mesh=mesh,
        in_specs=(tokens, tokens, tokens, tokens, P(), P()),
        out_specs=(tokens, tokens, tokens, tokens),
        check_vma=False,
    )
```

time: 651 us -> 123 us (0.19)
  matrix products: 301 us -> 0 us
  local copies, waits for them, and re-layouts: 135 us -> 5.85 us
  Pallas kernels: 0 us -> 116 us
  waiting for transfers between devices: 107 us -> 0 us
  starting transfers between devices: 48.4 us -> 0 us
  other arithmetic: 30 us -> 0 us
  loops' own time: 25.1 us -> 0 us
    dot_general x168 -> x0, matrix products: 301 us -> none  [the longest x24 103 us: spread_tiles(): jnp.einsum('tp,tkhd->pkhd', chooser, values, precision=lax.Precision.HIGH...]
    pallas_call x0 -> x1, Pallas kernels: none -> 116 us  [fused(): pl.pallas_call(functools.partial(fused_kernel, heads), out_shape=(tokens,...]
    all_to_all x8 -> x0, waiting for transfers between devices: 107 us -> none  [the longest x1 39.9 us: per_device(): lax.all_to_all(query, 'head', split_axis=1, concat_axis=0, tiled=True)]
    while x306 -> x0, local copies, waits for them, and re-layouts: 71.8 us -> none
    all_to_all x8 -> x0, starting transfers between devices: 32.1 us -> none  [the longest x1 5.95 us: per_device(): lax.all_to_all(key, 'head', split_axis=1, concat_axis=0, tiled=True)]
    convert_element_type x12 -> x0, local copies, waits for them, and re-layouts: 28.9 us -> none  [pick_tiles(): return picked.astype(pool.dtype)]
    another operation x3 -> x0, loops' own time: 25.1 us -> none  [the longest x1 9.84 us: per_device(): lax.fori_loop(0, busiest, backward_pass, (jnp.zeros(tile_shape, jnp.float...]
    ppermute x4 -> x0, starting transfers between devices: 16.2 us -> none  [the longest x2 7.18 us: passed_along(): return lax.ppermute(block, axis, route)]
  transfers between devices with their start and end apart: 12 -> 0, of which waited for: 8 -> 0; matrix products, arithmetic and copies ran while one was open for 4% -> 0% of each run, Pallas kernels for 0% -> 0%
where the time goes in v3:
time: 123 us; the launch traced here: 122 us
  Pallas kernels  116 us (94%)
  local copies, waits for them, and re-layouts  5.85 us (5%)
    pallas_call x1, Pallas kernels, fused(): pl.pallas_call(functools.partial(fused_kernel, heads), out_shape=(tokens,...  116 us
    unnamed x10, local copies, waits for them, and re-layouts  5.85 us

profile of v3, /device:TPU:1, one launch (start us, length us, event | category | flops | bytes accessed | tf_op | source)
XLA Modules:
  0.0 122.3 jit_solution(14967251008997224292)
XLA Ops:
  0.6 115.8 %fused.1 = (bf16[128,3072]{1,0:T(8,128)(2,1)}, bf16[128,3072]{1,0:T(8,128)(2,1)}, bf16[128,3072]{1,0:T(8,128)(2,1)}, bf16[128,3072]{1,0:T(8,128)(2,1)}) custom-call(s32[12,256]{1,0:T(8,128)} %bitcast.1, s32[256]{0:T(256)} %count_ref.1, bf16[128,3072]{1,0:T(8,128)(2,1)} %k_hbm.1, bf16[128,3072]{1,0:T(8,128)(2,1)} %v_hbm.1, bf16[128,3072]{1,0:T(8,128)(2,1)} %q_hbm.1, ...), custom_call_target="tpu_custom_call" | custom-call | tf_op jit(solution)/shard_map/fused/pallas_call | solution.py:401
  116.5 0.0 copy-start.2
  116.5 2.1 %copy.14 = bf16[128,3072]{1,0:T(8,128)(2,1)} copy(bf16[128,3072]{1,0:T(8,128)(2,1)} %get-tuple-element.8) | data formatting | bytes 1572864
  118.6 0.0 copy-done.2
  118.6 0.0 copy-start.1
  118.6 0.9 copy.15
  119.5 0.5 copy-done.1
  120.0 0.0 copy-start
  120.0 0.9 copy.16
  120.9 0.5 copy-done
  121.4 0.9 copy.17
Async XLA Ops:
  116.5 2.1 %copy-start.2 = (bf16[128,3072]{1,0:T(8,128)(2,1)S(1)}, bf16[128,3072]{1,0:T(8,128)(2,1)}, u32[]{:S(2)}) copy-start(bf16[128,3072]{1,0:T(8,128)(2,1)} %get-tuple-element.9) | copy-start | bytes 2359300
  118.6 1.4 %copy-start.1 = (bf16[128,3072]{1,0:T(8,128)(2,1)S(1)}, bf16[128,3072]{1,0:T(8,128)(2,1)}, u32[]{:S(2)}) copy-start(bf16[128,3072]{1,0:T(8,128)(2,1)} %get-tuple-element.10) | copy-start | bytes 2359300
  120.0 1.4 %copy-start = (bf16[128,3072]{1,0:T(8,128)(2,1)S(1)}, bf16[128,3072]{1,0:T(8,128)(2,1)}, u32[]{:S(2)}) copy-start(bf16[128,3072]{1,0:T(8,128)(2,1)} %get-tuple-element.11) | copy-start | bytes 2359300

commit v4 on v3

--- a/solution.py
+++ b/solution.py
@@ -60,7 +60,7 @@
     heads,
     list_ref, count_ref, k_hbm, v_hbm, q_hbm, g_hbm,
     o_out, dq_out, dk_out, dv_out,
-    kv_ref, q_ref, g_ref, acc_ref, mask_ref, w_ref, e_ref, dp_ref, stat_ref, ot_ref, dqt_ref,
+    kv_ref, q_ref, g_ref, acc_ref, mask_ref, e_ref, dp_ref, stat_ref,
     o_ref, dq_ref, dk_ref, dv_ref, low_ref, up_ref, from_below, from_above,
     local_sem, kv_recv, qg_recv, in_send, rim_recv, rim_send,
     out_local, out_send, out_recv, part_recv, part_send,
@@ -170,10 +170,10 @@
         tile = lax.rem(head + r, devices)
         part(i, 0, tile).wait_recv()
         part(i, 1, tile).wait_recv()
-        dv = acc_ref[i, TILES_DEV + tile, :, :HD] + (
+        dv = acc_ref[i, 0, TILES_DEV + tile] + (
             from_below[i, tile, 0].astype(jnp.float32) + from_above[i, tile, 0].astype(jnp.float32)
         )
-        dk = acc_ref[i, TILES_DEV + tile, :, HD:] + (
+        dk = acc_ref[i, 1, TILES_DEV + tile] + (
             from_below[i, tile, 1].astype(jnp.float32) + from_above[i, tile, 1].astype(jnp.float32)
         )
         dk_ref[i, tile] = (SCALING * dk).astype(jnp.bfloat16)
@@ -189,89 +189,73 @@
             result_local(2, i).start()
             result_local(3, i).start()
 
-    def service(i, r):
-        @pl.when(i < heads - 1)
-        def _():
-            forward(i + 1, r)
-
-        @pl.when(i == heads - 1)
-        def _():
-            finish(0, r)
-
     def attend(i, a, start, count):
         rows = count * TILE
-        w_ref[:TILE, :HD] = g_ref[i, a]
-        w_ref[TILE:, HD:] = q_ref[i, a]
+        queries = q_ref[i, pl.ds(a, 2)].reshape(2 * TILE, HD)
+        cotangents = g_ref[i, pl.ds(a, 2)].reshape(2 * TILE, HD)
+        nt, nn, tn = ((((x,), (y,)), ((), ())) for x, y in ((1, 1), (1, 0), (0, 0)))
+        dot = functools.partial(lax.dot_general, preferred_element_type=jnp.float32)
+        slots = [(f, u, f * TILES_DEV + start + u) for f in range(FRAMES) for u in range(count)]
 
         def pairs(f):
             first = f * TILES_DEV + start
             values = kv_ref[i, pl.ds(first, count), 0].reshape(rows, HD)
             keys = kv_ref[i, pl.ds(first, count), 1].reshape(rows, HD)
-            return first, values, keys
-
-        def scores(f, _):
-            first, values, keys = pairs(f)
-            both = lax.dot_general(
-                jnp.concatenate([values, keys], axis=1), w_ref[...], (((1,), (1,)), ((), ())),
-                preferred_element_type=jnp.float32,
-            )
-            grad_prob = both[:, :TILE]
-            score = both[:, TILE:]
-            extra = [mask_ref[a * POOL + first + u] for u in range(count)]
-            top = functools.reduce(
-                jnp.maximum,
-                [folded(jnp.maximum, score[u * TILE : (u + 1) * TILE]) - extra[u] for u in range(count)],
-            )
-            top = jnp.maximum(jnp.max(top, axis=0, keepdims=True), -0.1 * UNUSED)
-            total = jnp.zeros((8, TILE), jnp.float32)
-            dots = jnp.zeros((8, TILE), jnp.float32)
+            return values, keys
+
+        def tile(u):
+            return slice(u * TILE, (u + 1) * TILE)
+
+        for f in range(FRAMES):
+            values, keys = pairs(f)
+            scores = dot(keys, queries, nt)
+            grad_probs = dot(values, cotangents, nt)
             for u in range(count):
-                at = slice(u * TILE, (u + 1) * TILE)
-                e = jnp.exp2((score[at] - (top + extra[u])) * (SCALING * LOG2E))
-                e_ref[f, at] = e
-                total = total + folded(jnp.add, e)
-                dots = dots + folded(jnp.add, e * grad_prob[at])
-            dp_ref[f, :rows] = grad_prob
-            stat_ref[f, 0:1] = top
-            stat_ref[f, 1:2] = jnp.sum(total, axis=0, keepdims=True)
-            stat_ref[f, 2:3] = jnp.sum(dots, axis=0, keepdims=True)
-            return 0
-
-        lax.fori_loop(0, FRAMES, scores, 0)
-
-        top = functools.reduce(jnp.maximum, [stat_ref[f, 0:1] for f in range(FRAMES)])
-        weights = [jnp.exp2((stat_ref[f, 0:1] - top) * (SCALING * LOG2E)) for f in range(FRAMES)]
-        total = sum(weights[f] * stat_ref[f, 1:2] for f in range(FRAMES))
-        dots = sum(weights[f] * stat_ref[f, 2:3] for f in range(FRAMES))
+                n = f * count + u
+                score, grad_prob = scores[tile(u)], grad_probs[tile(u)]
+                top = jnp.max(folded(jnp.maximum, score), axis=0, keepdims=True)
+                e = jnp.exp2((score - top) * (SCALING * LOG2E))
+                e_ref[n] = e
+                dp_ref[n] = grad_prob
+                stat_ref[n, 0:1] = top
+                stat_ref[n, 1:2] = jnp.sum(folded(jnp.add, e), axis=0, keepdims=True)
+                stat_ref[n, 2:3] = jnp.sum(folded(jnp.add, e * grad_prob), axis=0, keepdims=True)
+
+        left = lax.broadcasted_iota(jnp.int32, (1, 2 * TILE), 1) < TILE
+        tops = [
+            stat_ref[n, 0:1] - jnp.where(left, mask_ref[a * POOL + slot], mask_ref[(a + 1) * POOL + slot])
+            for n, (_, _, slot) in enumerate(slots)
+        ]
+        top = functools.reduce(jnp.maximum, tops)
+        weights = [jnp.exp2((t - top) * (SCALING * LOG2E)) for t in tops]
+        total = sum(w * stat_ref[n, 1:2] for n, w in enumerate(weights))
+        delta = sum(w * stat_ref[n, 2:3] for n, w in enumerate(weights)) / total
         inverse = 1.0 / total
+        for n, weight in enumerate(weights):
+            stat_ref[n, 3:4] = weight * inverse
+
+        out = jnp.zeros((HD, 2 * TILE), jnp.float32)
+        dq = jnp.zeros((HD, 2 * TILE), jnp.float32)
         for f in range(FRAMES):
-            stat_ref[f, 3:4] = weights[f] * inverse
-            stat_ref[f, 4:5] = dots * inverse
-        ot_ref[...] = jnp.zeros_like(ot_ref)
-        dqt_ref[...] = jnp.zeros_like(dqt_ref)
-
-        def grads(f, _):
-            first, values, keys = pairs(f)
-            p = e_ref[f, :rows] * stat_ref[f, 3:4]
-            ds = (p * (dp_ref[f, :rows] - stat_ref[f, 4:5])).astype(jnp.bfloat16)
-            pb = p.astype(jnp.bfloat16)
-            both = lax.dot_general(
-                jnp.concatenate([pb, ds], axis=1), w_ref[...], (((1,), (0,)), ((), ())),
-                preferred_element_type=jnp.float32,
-            )
+            values, keys = pairs(f)
+            probs, grad_scores = [], []
             for u in range(count):
-                acc_ref[i, first + u] += both[u * TILE : (u + 1) * TILE]
-            ot_ref[...] += lax.dot_general(
-                values, pb, (((0,), (0,)), ((), ())), preferred_element_type=jnp.float32
-            )
-            dqt_ref[...] += lax.dot_general(
-                keys, ds, (((0,), (0,)), ((), ())), preferred_element_type=jnp.float32
-            )
-            return 0
-
-        lax.fori_loop(0, FRAMES, grads, 0)
-        o_ref[i, a] = ot_ref[...].T.astype(jnp.bfloat16)
-        dq_ref[i, a] = (dqt_ref[...].T * SCALING).astype(jnp.bfloat16)
+                n = f * count + u
+                p = e_ref[n] * stat_ref[n, 3:4]
+                probs.append(p.astype(jnp.bfloat16))
+                grad_scores.append((p * (dp_ref[n] - delta)).astype(jnp.bfloat16))
+            pb = jnp.concatenate(probs, axis=0)
+            ds = jnp.concatenate(grad_scores, axis=0)
+            dv = dot(pb, cotangents, nn)
+            dk = dot(ds, queries, nn)
+            for u in range(count):
+                slot = f * TILES_DEV + start + u
+                acc_ref[i, 0, slot] += dv[tile(u)]
+                acc_ref[i, 1, slot] += dk[tile(u)]
+            out = out + dot(values, pb, tn)
+            dq = dq + dot(keys, ds, tn)
+        o_ref[i, pl.ds(a, 2)] = out.T.astype(jnp.bfloat16).reshape(2, TILE, HD)
+        dq_ref[i, pl.ds(a, 2)] = (dq.T * SCALING).astype(jnp.bfloat16).reshape(2, TILE, HD)
 
     for i in range(heads):
         for x in range(4):
@@ -297,7 +281,6 @@
         return 0
 
     lax.fori_loop(0, TILES_DEV, masks, 0)
-    w_ref[...] = jnp.zeros_like(w_ref)
 
     def first_tiles(r, _):
         forward(0, r)
@@ -310,7 +293,8 @@
 
     def head_step(i, _):
         def clear(slot, _):
-            acc_ref[i, slot] = jnp.zeros((TILE, 2 * HD), jnp.float32)
+            for kind in range(2):
+                acc_ref[i, kind, slot] = jnp.zeros((TILE, HD), jnp.float32)
             return 0
 
         lax.fori_loop(0, POOL, clear, 0)
@@ -323,6 +307,18 @@
         def _():
             send(i + 2, (0, 1))
 
+        def ahead(r, _):
+            @pl.when(i < heads - 1)
+            def _():
+                forward(i + 1, r)
+
+            @pl.when(i == heads - 1)
+            def _():
+                finish(0, lax.rem(r + 1, devices))
+
+            return 0
+
+        lax.fori_loop(0, devices, ahead, 0)
         for x in (2, 3):
             local(x, i).wait()
             whole(q_ref.at[i, others], in_send.at[i, x], qg_recv.at[i, x - 2]).wait_recv()
@@ -332,26 +328,22 @@
             ).wait_recv()
 
         def outer(n, _):
-            half = lax.div(n, 2)
-            attend(i, n + 4 * half, 4 * half, 4)
-            service(i, n)
+            attend(i, 6 * n, 4 * n, 4)
             return 0
 
         def inner(n, _):
-            attend(i, n + 2, 2 * lax.div(n, 2), 6)
-            service(i, n + 4)
-            return 0
-
-        lax.fori_loop(0, 4, outer, 0)
-        lax.fori_loop(0, 4, inner, 0)
+            attend(i, 2 * n + 2, 2 * n, 6)
+            return 0
+
+        lax.fori_loop(0, 2, outer, 0)
+        lax.fori_loop(0, 2, inner, 0)
 
         def leave(r, _):
             for side, (ref, (_, h)) in enumerate(((up_ref, above), (low_ref, below))):
                 tile = lax.rem(h + 1 + r, devices)
                 for kind in range(2):
-                    ref[i, tile, kind] = acc_ref[
-                        i, 2 * TILES_DEV * (1 - side) + tile, :, kind * HD : (kind + 1) * HD
-                    ].astype(jnp.bfloat16)
+                    slot = 2 * TILES_DEV * (1 - side) + tile
+                    ref[i, tile, kind] = acc_ref[i, kind, slot].astype(jnp.bfloat16)
                 part(i, side, tile).start()
             return 0
 
@@ -407,14 +399,11 @@
             pltpu.VMEM((heads, POOL, 2, TILE, HD), jnp.bfloat16),
             tiles,
             tiles,
-            pltpu.VMEM((heads, POOL, TILE, 2 * HD), jnp.float32),
+            pltpu.VMEM((heads, 2, POOL, TILE, HD), jnp.float32),
             pltpu.SMEM((TILES_DEV * POOL,), jnp.float32),
-            pltpu.VMEM((2 * TILE, 2 * HD), jnp.bfloat16),
-            pltpu.VMEM((FRAMES, 6 * TILE, TILE), jnp.float32),
-            pltpu.VMEM((FRAMES, 6 * TILE, TILE), jnp.float32),
-            pltpu.VMEM((FRAMES, 8, TILE), jnp.float32),
-            pltpu.VMEM((HD, TILE), jnp.float32),
-            pltpu.VMEM((HD, TILE), jnp.float32),
+            pltpu.VMEM((6 * FRAMES, TILE, 2 * TILE), jnp.float32),
+            pltpu.VMEM((6 * FRAMES, TILE, 2 * TILE), jnp.float32),
+            pltpu.VMEM((6 * FRAMES, 8, 2 * TILE), jnp.float32),
             tiles,
             tiles,
             tiles,
@@ -442,8 +431,27 @@
     )(tile_list, tile_count, key, value, query, cotangent)
 
 
+def emit_kernel(*refs):
+    count = len(refs) // 2
+    for n in range(count):
+        refs[count + n][...] = refs[n][...]
+
+
+def emit(arrays):
+    rows, columns = arrays[0].shape
+    spec = pl.BlockSpec((rows // 8, columns), lambda n: (n, 0))
+    return pl.pallas_call(
+        emit_kernel,
+        grid=(8,),
+        out_shape=tuple(jax.ShapeDtypeStruct(a.shape, a.dtype) for a in arrays),
+        in_specs=[spec] * len(arrays),
+        out_specs=(spec,) * len(arrays),
+        name="emit",
+    )(*arrays)
+
+
 def per_device(query, key, value, grad_out, tile_list, tile_count):
-    return tuple(fused(tile_list.T, tile_count, key, value, query, grad_out))
+    return tuple(emit(fused(tile_list.T, tile_count, key, value, query, grad_out)))
 
 
 def solution(mesh):

time: 123 us -> 104 us (0.85)
  Pallas kernels: 116 us -> 103 us
  local copies, waits for them, and re-layouts: 5.85 us -> 0 us
    pallas_call x1, Pallas kernels: 116 us -> 96.2 us  [fused(): pl.pallas_call(functools.partial(fused_kernel, heads), out_shape=(tokens,...]
    pallas_call x0 -> x1, Pallas kernels: none -> 6.26 us  [emit(): pl.pallas_call(emit_kernel, grid=(8,), out_shape=tuple((jax.ShapeDtypeStr...]
    unnamed x10 -> x0, local copies, waits for them, and re-layouts: 5.85 us -> none
where the time goes in v4:
time: 104 us; the launch traced here: 103 us
  Pallas kernels  103 us (99%)
    pallas_call x1, Pallas kernels, fused(): pl.pallas_call(functools.partial(fused_kernel, heads), out_shape=(tokens,...  96.2 us
    pallas_call x1, Pallas kernels, emit(): pl.pallas_call(emit_kernel, grid=(8,), out_shape=tuple((jax.ShapeDtypeStr...  6.26 us

profile of v4, /device:TPU:1, one launch (start us, length us, event | category | flops | bytes accessed | tf_op | source)
XLA Modules:
  0.0 103.1 jit_solution(1232557978114027855)
XLA Ops:
  0.6 96.2 %fused.1 = (bf16[128,3072]{1,0:T(8,128)(2,1)}, bf16[128,3072]{1,0:T(8,128)(2,1)}, bf16[128,3072]{1,0:T(8,128)(2,1)}, bf16[128,3072]{1,0:T(8,128)(2,1)}) custom-call(s32[12,256]{1,0:T(8,128)} %bitcast.1, s32[256]{0:T(256)} %count_ref.1, bf16[128,3072]{1,0:T(8,128)(2,1)} %k_hbm.1, bf16[128,3072]{1,0:T(8,128)(2,1)} %v_hbm.1, bf16[128,3072]{1,0:T(8,128)(2,1)} %q_hbm.1, ...), custom_call_target="tpu_custom_call" | custom-call | tf_op jit(solution)/shard_map/fused/pallas_call | solution.py:393
  96.9 6.3 %emit.1 = (bf16[128,3072]{1,0:T(8,128)(2,1)}, bf16[128,3072]{1,0:T(8,128)(2,1)}, bf16[128,3072]{1,0:T(8,128)(2,1)}, bf16[128,3072]{1,0:T(8,128)(2,1)}) custom-call(bf16[128,3072]{1,0:T(8,128)(2,1)} %get-tuple-element.8.refs_0_, bf16[128,3072]{1,0:T(8,128)(2,1)} %get-tuple-element.9.refs_1_, bf16[128,3072]{1,0:T(8,128)(2,1)} %get-tuple-element.10.refs_2_, ...), custom_call_target="tpu_custom_call" | custom-call | tf_op jit(solution)/shard_map/emit/pallas_call | solution.py:443

commit v5 on v4

--- a/solution.py
+++ b/solution.py
@@ -150,21 +150,39 @@
 
         peers(both)
 
-    def forward(i, r):
-        tile = lax.rem(head + r, devices)
-
-        @pl.when(r == 0)
-        def _():
-            local(0, i).wait()
-            local(1, i).wait()
-
-        @pl.when(r > 0)
-        def _():
-            incoming(0, i, tile, tile).wait_recv()
-            incoming(1, i, tile, tile).wait_recv()
-
+    def pass_on(i, tile):
         rim(i, 0, tile).start()
         rim(i, 1, tile).start()
+
+    def forward_own(i):
+        local(0, i).wait()
+        local(1, i).wait()
+        pass_on(i, head)
+
+    def forward(i):
+        def arrived(peer):
+            incoming(0, i, peer, peer).wait_recv()
+            incoming(1, i, peer, peer).wait_recv()
+            pass_on(i, peer)
+
+        peers(arrived)
+
+    def forward_halves():
+        for x in range(2):
+
+            def arrived(peer):
+                incoming(x, 0, peer, peer).wait_recv()
+                for side, (s, h) in enumerate((above, below)):
+                    pltpu.make_async_remote_copy(
+                        src_ref=kv_ref.at[0, TILES_DEV + peer, x],
+                        dst_ref=kv_ref.at[0, 2 * TILES_DEV * side + peer, x],
+                        send_sem=rim_send.at[0, side],
+                        recv_sem=rim_recv.at[0, side],
+                        device_id={"seq": s, "head": h},
+                        device_id_type=MESH,
+                    ).start()
+
+            peers(arrived)
 
     def finish(i, r):
         tile = lax.rem(head + r, devices)
@@ -261,9 +279,14 @@
         for x in range(4):
             local(x, i).start()
     entry_barrier(slab, head, devices, (above, below))
-    send(0, (0, 1))
-    forward(0, 0)
-    send(0, (2, 3))
+    send(0, (0,))
+    send(0, (1,))
+    for i in range(heads):
+        forward_own(i)
+    for i in range(1, heads):
+        send(i, (0, 1))
+    for i in range(heads):
+        send(i, (2, 3))
 
     def masks(a, _):
         used = count_ref[slab * TILES_DEV + a]
@@ -282,16 +305,37 @@
 
     lax.fori_loop(0, TILES_DEV, masks, 0)
 
-    def first_tiles(r, _):
-        forward(0, r)
-        return 0
-
-    lax.fori_loop(1, devices, first_tiles, 0)
-    send(1, (0, 1))
+    forward_halves()
+    for i in range(1, heads):
+        forward(i)
 
     others = pl.ds(0, devices - 1)
 
+    def leave(i):
+        def parts(r, _):
+            for side, (ref, (_, h)) in enumerate(((up_ref, above), (low_ref, below))):
+                tile = lax.rem(h + 1 + r, devices)
+                slot = 2 * TILES_DEV * (1 - side) + tile
+                for kind in range(2):
+                    ref[i, tile, kind] = acc_ref[i, kind, slot].astype(jnp.bfloat16)
+                part(i, side, tile).start()
+            return 0
+
+        lax.fori_loop(0, devices, parts, 0)
+
+        def both(peer):
+            result(0, i, peer).start()
+            result(1, i, peer).start()
+
+        peers(both)
+        result_local(0, i).start()
+        result_local(1, i).start()
+
     def head_step(i, _):
+        @pl.when(i > 0)
+        def _():
+            leave(i - 1)
+
         def clear(slot, _):
             for kind in range(2):
                 acc_ref[i, kind, slot] = jnp.zeros((TILE, HD), jnp.float32)
@@ -299,26 +343,6 @@
 
         lax.fori_loop(0, POOL, clear, 0)
 
-        @pl.when(i < heads - 1)
-        def _():
-            send(i + 1, (2, 3))
-
-        @pl.when(i < heads - 2)
-        def _():
-            send(i + 2, (0, 1))
-
-        def ahead(r, _):
-            @pl.when(i < heads - 1)
-            def _():
-                forward(i + 1, r)
-
-            @pl.when(i == heads - 1)
-            def _():
-                finish(0, lax.rem(r + 1, devices))
-
-            return 0
-
-        lax.fori_loop(0, devices, ahead, 0)
         for x in (2, 3):
             local(x, i).wait()
             whole(q_ref.at[i, others], in_send.at[i, x], qg_recv.at[i, x - 2]).wait_recv()
@@ -337,35 +361,16 @@
 
         lax.fori_loop(0, 2, outer, 0)
         lax.fori_loop(0, 2, inner, 0)
-
-        def leave(r, _):
-            for side, (ref, (_, h)) in enumerate(((up_ref, above), (low_ref, below))):
-                tile = lax.rem(h + 1 + r, devices)
-                for kind in range(2):
-                    slot = 2 * TILES_DEV * (1 - side) + tile
-                    ref[i, tile, kind] = acc_ref[i, kind, slot].astype(jnp.bfloat16)
-                part(i, side, tile).start()
-            return 0
-
-        lax.fori_loop(0, devices, leave, 0)
-
-        def both(peer):
-            result(0, i, peer).start()
-            result(1, i, peer).start()
-
-        peers(both)
-        result_local(0, i).start()
-        result_local(1, i).start()
         return 0
 
     lax.fori_loop(0, heads, head_step, 0)
+    leave(heads - 1)
 
     def last(n, _):
-        i = 1 + lax.div(n, devices)
-        finish(i, lax.rem(n + 1, devices))
+        finish(lax.div(n, devices), lax.rem(n + 1, devices))
         return 0
 
-    lax.fori_loop(0, (heads - 1) * devices, last, 0)
+    lax.fori_loop(0, heads * devices, last, 0)
 
     def settle(i, _):
         for x in range(4):
@@ -392,7 +397,7 @@
     dma = pltpu.SemaphoreType.DMA
     return pl.pallas_call(
         functools.partial(fused_kernel, heads),
-        out_shape=(tokens,) * 4,
+        out_shape=(pltpu.VMEM(key.shape, jnp.bfloat16),) * 4,
         in_specs=[smem, smem, hbm, hbm, hbm, hbm],
         out_specs=(hbm,) * 4,
         scratch_shapes=[
@@ -425,7 +430,7 @@
             dma((heads, 2)),
         ],
         compiler_params=pltpu.CompilerParams(
-            collective_id=0, has_side_effects=True, vmem_limit_bytes=58 * 2**20
+            collective_id=0, has_side_effects=True, vmem_limit_bytes=36 * 2**20
         ),
         name="fused",
     )(tile_list, tile_count, key, value, query, cotangent)
@@ -433,25 +438,33 @@
 
 def emit_kernel(*refs):
     count = len(refs) // 2
-    for n in range(count):
-        refs[count + n][...] = refs[n][...]
+    sem = refs[-1]
+    stores = [pltpu.make_async_copy(refs[n], refs[count + n], sem.at[n]) for n in range(count)]
+    for store in stores:
+        store.start()
+    for store in stores:
+        store.wait()
 
 
 def emit(arrays):
-    rows, columns = arrays[0].shape
-    spec = pl.BlockSpec((rows // 8, columns), lambda n: (n, 0))
+    hbm = pl.BlockSpec(memory_space=pl.ANY)
+    arrays = [pltpu.with_memory_space_constraint(a, pltpu.VMEM) for a in arrays]
     return pl.pallas_call(
         emit_kernel,
-        grid=(8,),
-        out_shape=tuple(jax.ShapeDtypeStruct(a.shape, a.dtype) for a in arrays),
-        in_specs=[spec] * len(arrays),
-        out_specs=(spec,) * len(arrays),
+        out_shape=tuple(pltpu.HBM(a.shape, a.dtype) for a in arrays),
+        in_specs=[hbm] * len(arrays),
+        out_specs=(hbm,) * len(arrays),
+        scratch_shapes=[pltpu.SemaphoreType.DMA((len(arrays),))],
         name="emit",
     )(*arrays)
 
 
 def per_device(query, key, value, grad_out, tile_list, tile_count):
-    return tuple(emit(fused(tile_list.T, tile_count, key, value, query, grad_out)))
+    tile_list, tile_count, query, key, value, grad_out = (
+        pltpu.with_memory_space_constraint(x, pltpu.HBM)
+        for x in (tile_list.T, tile_count, query, key, value, grad_out)
+    )
+    return tuple(emit(fused(tile_list, tile_count, key, value, query, grad_out)))
 
 
 def solution(mesh):

time: 104 us -> 87.1 us (0.84)
  Pallas kernels: 103 us -> 86.3 us
    pallas_call x2, Pallas kernels: 103 us -> 86.3 us  [the longest x1 84.6 us: fused(): pl.pallas_call(functools.partial(fused_kernel, heads), out_shape=(pltpu.V...]
where the time goes in v5:
time: 87.1 us; the launch traced here: 86.9 us
  Pallas kernels  86.3 us (99%)
    pallas_call x1, Pallas kernels, fused(): pl.pallas_call(functools.partial(fused_kernel, heads), out_shape=(pltpu.V...  84.6 us

profile of v5, /device:TPU:1, one launch (start us, length us, event | category | flops | bytes accessed | tf_op | source)
XLA Modules:
  0.0 86.9 jit_solution(12936868595649542612)
XLA Ops:
  0.6 84.6 %fused.1 = (bf16[128,3072]{1,0:T(8,128)(2,1)S(1)}, bf16[128,3072]{1,0:T(8,128)(2,1)S(1)}, bf16[128,3072]{1,0:T(8,128)(2,1)S(1)}, bf16[128,3072]{1,0:T(8,128)(2,1)S(1)}) custom-call(s32[12,256]{1,0:T(8,128)} %bitcast.1, s32[256]{0:T(256)} %count_ref.1, bf16[128,3072]{1,0:T(8,128)(2,1)} %k_hbm.1, bf16[128,3072]{1,0:T(8,128)(2,1)} %v_hbm.1, ...), custom_call_target="tpu_custom_call" | custom-call | tf_op jit(solution)/shard_map/fused/pallas_call | solution.py:398
  85.2 1.7 %emit.1 = (bf16[128,3072]{1,0:T(8,128)(2,1)}, bf16[128,3072]{1,0:T(8,128)(2,1)}, bf16[128,3072]{1,0:T(8,128)(2,1)}, bf16[128,3072]{1,0:T(8,128)(2,1)}) custom-call(bf16[128,3072]{1,0:T(8,128)(2,1)S(1)} %get-tuple-element.8.refs_0_, bf16[128,3072]{1,0:T(8,128)(2,1)S(1)} %get-tuple-element.9.refs_1_, bf16[128,3072]{1,0:T(8,128)(2,1)S(1)} %get-tuple-element.10.refs_2_, ...), custom_call_target="tpu_custom_call" | custom-call | tf_op jit(solution)/shard_map/emit/pallas_call | solution.py:452

commit v6 on v5

--- a/solution.py
+++ b/solution.py
@@ -37,7 +37,7 @@
     return slab, head, own, (above, head_above), (below, head_below)
 
 
-def entry_barrier(slab, head, devices, neighbours):
+def greet_all(slab, head, devices, neighbours):
     barrier = pltpu.get_barrier_semaphore()
 
     def greet(r, _):
@@ -49,7 +49,7 @@
     lax.fori_loop(1, devices, greet, 0)
     for s, h in neighbours:
         pl.semaphore_signal(barrier, inc=1, device_id={"seq": s, "head": h}, device_id_type=MESH)
-    pl.semaphore_wait(barrier, devices - 1 + len(neighbours))
+    return barrier, devices - 1 + len(neighbours)
 
 
 def folded(op, rows):
@@ -275,10 +275,11 @@
         o_ref[i, pl.ds(a, 2)] = out.T.astype(jnp.bfloat16).reshape(2, TILE, HD)
         dq_ref[i, pl.ds(a, 2)] = (dq.T * SCALING).astype(jnp.bfloat16).reshape(2, TILE, HD)
 
-    for i in range(heads):
-        for x in range(4):
+    barrier, greetings = greet_all(slab, head, devices, (above, below))
+    for x in range(4):
+        for i in range(heads):
             local(x, i).start()
-    entry_barrier(slab, head, devices, (above, below))
+    pl.semaphore_wait(barrier, greetings)
     send(0, (0,))
     send(0, (1,))
     for i in range(heads):
@@ -351,12 +352,20 @@
                 kv_ref.at[i, pl.ds(TILES_DEV, TILES_DEV)], rim_send.at[i, side], rim_recv.at[i, side]
             ).wait_recv()
 
+        def first_finish(r):
+            @pl.when(i == heads - 1)
+            def _():
+                finish(0, lax.rem(r + 1, devices))
+                finish(0, lax.rem(r + 2, devices))
+
         def outer(n, _):
             attend(i, 6 * n, 4 * n, 4)
+            first_finish(2 * n)
             return 0
 
         def inner(n, _):
             attend(i, 2 * n + 2, 2 * n, 6)
+            first_finish(2 * n + 4)
             return 0
 
         lax.fori_loop(0, 2, outer, 0)
@@ -366,25 +375,32 @@
     lax.fori_loop(0, heads, head_step, 0)
     leave(heads - 1)
 
-    def last(n, _):
-        finish(lax.div(n, devices), lax.rem(n + 1, devices))
-        return 0
-
-    lax.fori_loop(0, heads * devices, last, 0)
-
-    def settle(i, _):
+    def settle_arrivals(i, _):
         for x in range(4):
-            result_local(x, i).wait()
-            whole(q_ref.at[i, others], out_send.at[i, x], out_recv.at[i, x]).wait()
             whole(q_ref.at[i, others], in_send.at[i, x], out_recv.at[i, x]).wait_send()
         for side in range(2):
             whole(
                 kv_ref.at[i, pl.ds(TILES_DEV, TILES_DEV)], rim_send.at[i, side], rim_recv.at[i, side]
             ).wait_send()
+        return 0
+
+    lax.fori_loop(0, heads, settle_arrivals, 0)
+
+    def last(n, _):
+        finish(1 + lax.div(n, devices), lax.rem(n + 1, devices))
+        return 0
+
+    lax.fori_loop(0, (heads - 1) * devices, last, 0)
+
+    def settle_results(i, _):
+        for x in range(4):
+            result_local(x, i).wait()
+            whole(q_ref.at[i, others], out_send.at[i, x], out_recv.at[i, x]).wait()
+        for side in range(2):
             whole(low_ref.at[i], part_send.at[i, side], part_recv.at[i, side, 0]).wait_send()
         return 0
 
-    lax.fori_loop(0, heads, settle, 0)
+    lax.fori_loop(0, heads, settle_results, 0)
 
 
 def fused(tile_list, tile_count, key, value, query, cotangent):

time: 87.1 us -> 86.5 us (level)
  no operation moved by 1% of the time
where the time goes in v6:
time: 86.5 us; the launch traced here: 86.4 us
  Pallas kernels  85.7 us (99%)
    pallas_call x1, Pallas kernels, fused(): pl.pallas_call(functools.partial(fused_kernel, heads), out_shape=(pltpu.V...  84 us

profile of v6, /device:TPU:1, one launch (start us, length us, event | category | flops | bytes accessed | tf_op | source)
XLA Modules:
  0.0 86.4 jit_solution(11286975807152454529)
XLA Ops:
  0.6 84.0 %fused.1 = (bf16[128,3072]{1,0:T(8,128)(2,1)S(1)}, bf16[128,3072]{1,0:T(8,128)(2,1)S(1)}, bf16[128,3072]{1,0:T(8,128)(2,1)S(1)}, bf16[128,3072]{1,0:T(8,128)(2,1)S(1)}) custom-call(s32[12,256]{1,0:T(8,128)} %bitcast.1, s32[256]{0:T(256)} %count_ref.1, bf16[128,3072]{1,0:T(8,128)(2,1)} %k_hbm.1, bf16[128,3072]{1,0:T(8,128)(2,1)} %v_hbm.1, ...), custom_call_target="tpu_custom_call" | custom-call | tf_op jit(solution)/shard_map/fused/pallas_call | solution.py:414
  84.7 1.7 %emit.1 = (bf16[128,3072]{1,0:T(8,128)(2,1)}, bf16[128,3072]{1,0:T(8,128)(2,1)}, bf16[128,3072]{1,0:T(8,128)(2,1)}, bf16[128,3072]{1,0:T(8,128)(2,1)}) custom-call(bf16[128,3072]{1,0:T(8,128)(2,1)S(1)} %get-tuple-element.8.refs_0_, bf16[128,3072]{1,0:T(8,128)(2,1)S(1)} %get-tuple-element.9.refs_1_, bf16[128,3072]{1,0:T(8,128)(2,1)S(1)} %get-tuple-element.10.refs_2_, ...), custom_call_target="tpu_custom_call" | custom-call | tf_op jit(solution)/shard_map/emit/pallas_call | solution.py:468

commit v7 on v6

--- a/solution.py
+++ b/solution.py
@@ -58,9 +58,9 @@
 
 def fused_kernel(
     heads,
-    list_ref, count_ref, k_hbm, v_hbm, q_hbm, g_hbm,
+    list_hbm, count_hbm, k_hbm, v_hbm, q_hbm, g_hbm,
     o_out, dq_out, dk_out, dv_out,
-    kv_ref, q_ref, g_ref, acc_ref, mask_ref, e_ref, dp_ref, stat_ref,
+    list_ref, count_ref, table_sem, kv_ref, q_ref, g_ref, acc_ref, mask_ref, e_ref, dp_ref, stat_ref,
     o_ref, dq_ref, dk_ref, dv_ref, low_ref, up_ref, from_below, from_above,
     local_sem, kv_recv, qg_recv, in_send, rim_recv, rim_send,
     out_local, out_send, out_recv, part_recv, part_send,
@@ -279,6 +279,12 @@
     for x in range(4):
         for i in range(heads):
             local(x, i).start()
+    tables = [
+        pltpu.make_async_copy(list_hbm, list_ref, table_sem.at[0]),
+        pltpu.make_async_copy(count_hbm, count_ref, table_sem.at[1]),
+    ]
+    for table in tables:
+        table.start()
     pl.semaphore_wait(barrier, greetings)
     send(0, (0,))
     send(0, (1,))
@@ -289,6 +295,9 @@
     for i in range(heads):
         send(i, (2, 3))
 
+    for table in tables:
+        table.wait()
+
     def masks(a, _):
         used = count_ref[slab * TILES_DEV + a]
         listed = [
@@ -406,7 +415,6 @@
 def fused(tile_list, tile_count, key, value, query, cotangent):
     heads = key.shape[1] // (TILES_DEV * HD)
     hbm = pl.BlockSpec(memory_space=pl.ANY)
-    smem = pl.BlockSpec(memory_space=pltpu.SMEM)
     tokens = jax.ShapeDtypeStruct(key.shape, jnp.bfloat16)
     tiles = pltpu.VMEM((heads, TILES_DEV, TILE, HD), jnp.bfloat16)
     pairs = pltpu.VMEM((heads, TILES_DEV, 2, TILE, HD), jnp.bfloat16)
@@ -414,9 +422,12 @@
     return pl.pallas_call(
         functools.partial(fused_kernel, heads),
         out_shape=(pltpu.VMEM(key.shape, jnp.bfloat16),) * 4,
-        in_specs=[smem, smem, hbm, hbm, hbm, hbm],
+        in_specs=[hbm] * 6,
         out_specs=(hbm,) * 4,
         scratch_shapes=[
+            pltpu.SMEM(tile_list.shape, jnp.int32),
+            pltpu.SMEM(tile_count.shape, jnp.int32),
+            dma((2,)),
             pltpu.VMEM((heads, POOL, 2, TILE, HD), jnp.bfloat16),
             tiles,
             tiles,

time: 86.5 us -> 85.4 us (0.987)
  Pallas kernels: 85.7 us -> 84.7 us
    pallas_call x1, Pallas kernels: 84 us -> 83 us  [fused(): pl.pallas_call(functools.partial(fused_kernel, heads), out_shape=(pltpu.V...]
where the time goes in v7:
time: 85.4 us
  Pallas kernels  84.7 us (99%)
    pallas_call x1, Pallas kernels, fused(): pl.pallas_call(functools.partial(fused_kernel, heads), out_shape=(pltpu.V...  83 us

profile of v7, /device:TPU:1, one launch (start us, length us, event | category | flops | bytes accessed | tf_op | source)
XLA Modules:
  0.0 85.4 jit_solution(8998486113261198654)
XLA Ops:
  0.6 83.0 %fused.1 = (bf16[128,3072]{1,0:T(8,128)(2,1)S(1)}, bf16[128,3072]{1,0:T(8,128)(2,1)S(1)}, bf16[128,3072]{1,0:T(8,128)(2,1)S(1)}, bf16[128,3072]{1,0:T(8,128)(2,1)S(1)}) custom-call(s32[12,256]{1,0:T(8,128)} %bitcast.1, s32[256]{0:T(256)} %count_hbm.1, bf16[128,3072]{1,0:T(8,128)(2,1)} %k_hbm.1, bf16[128,3072]{1,0:T(8,128)(2,1)} %v_hbm.1, ...), custom_call_target="tpu_custom_call" | custom-call | tf_op jit(solution)/shard_map/fused/pallas_call | solution.py:422
  83.7 1.7 %emit.1 = (bf16[128,3072]{1,0:T(8,128)(2,1)}, bf16[128,3072]{1,0:T(8,128)(2,1)}, bf16[128,3072]{1,0:T(8,128)(2,1)}, bf16[128,3072]{1,0:T(8,128)(2,1)}) custom-call(bf16[128,3072]{1,0:T(8,128)(2,1)S(1)} %get-tuple-element.8.refs_0_, bf16[128,3072]{1,0:T(8,128)(2,1)S(1)} %get-tuple-element.9.refs_1_, bf16[128,3072]{1,0:T(8,128)(2,1)S(1)} %get-tuple-element.10.refs_2_, ...), custom_call_target="tpu_custom_call" | custom-call | tf_op jit(solution)/shard_map/emit/pallas_call | solution.py:479

commit v8 on v7

--- a/solution.py
+++ b/solution.py
@@ -292,8 +292,12 @@
         forward_own(i)
     for i in range(1, heads):
         send(i, (0, 1))
+
+    forward_halves()
     for i in range(heads):
         send(i, (2, 3))
+    for i in range(1, heads):
+        forward(i)
 
     for table in tables:
         table.wait()
@@ -315,9 +319,6 @@
 
     lax.fori_loop(0, TILES_DEV, masks, 0)
 
-    forward_halves()
-    for i in range(1, heads):
-        forward(i)
 
     others = pl.ds(0, devices - 1)
 

time: 85.4 us -> 85.4 us (level)
  no operation moved by 1% of the time
where the time goes in v8:
time: 85.4 us
  Pallas kernels  84.7 us (99%)
    pallas_call x1, Pallas kernels, fused(): pl.pallas_call(functools.partial(fused_kernel, heads), out_shape=(pltpu.V...  83 us

profile of v8, /device:TPU:1, one launch (start us, length us, event | category | flops | bytes accessed | tf_op | source)
XLA Modules:
  0.0 85.4 jit_solution(13396234711803052937)
XLA Ops:
  0.6 83.0 %fused.1 = (bf16[128,3072]{1,0:T(8,128)(2,1)S(1)}, bf16[128,3072]{1,0:T(8,128)(2,1)S(1)}, bf16[128,3072]{1,0:T(8,128)(2,1)S(1)}, bf16[128,3072]{1,0:T(8,128)(2,1)S(1)}) custom-call(s32[12,256]{1,0:T(8,128)} %bitcast.1, s32[256]{0:T(256)} %count_hbm.1, bf16[128,3072]{1,0:T(8,128)(2,1)} %k_hbm.1, bf16[128,3072]{1,0:T(8,128)(2,1)} %v_hbm.1, ...), custom_call_target="tpu_custom_call" | custom-call | tf_op jit(solution)/shard_map/fused/pallas_call | solution.py:423
  83.7 1.7 %emit.1 = (bf16[128,3072]{1,0:T(8,128)(2,1)}, bf16[128,3072]{1,0:T(8,128)(2,1)}, bf16[128,3072]{1,0:T(8,128)(2,1)}, bf16[128,3072]{1,0:T(8,128)(2,1)}) custom-call(bf16[128,3072]{1,0:T(8,128)(2,1)S(1)} %get-tuple-element.8.refs_0_, bf16[128,3072]{1,0:T(8,128)(2,1)S(1)} %get-tuple-element.9.refs_1_, bf16[128,3072]{1,0:T(8,128)(2,1)S(1)} %get-tuple-element.10.refs_2_, ...), custom_call_target="tpu_custom_call" | custom-call | tf_op jit(solution)/shard_map/emit/pallas_call | solution.py:480
